TPU v7x, 32 devices: a whole 2x2x4 slice. The times are simulated.
32 devices in a mesh: band: 16 (over z, x, core), lev: 2 (over y).
Axes of the slice: x: 2, y: 2, z: 4, core: 2. Of those that a mesh axis runs over, the one named last changes fastest.
Arguments:
- air_heat_state: bfloat16 [8, 2, 512, 4096], P('lev', None, 'band'), may hold values from -6 to 6
- mixing_coefficient: bfloat16 [2, 512, 4096], P(None, 'band'), may hold values from 0.049804688 to 0.19921875
- layer_depth_factor: float32 [8], P('lev'), may hold values from 0.3 to 0.8
- weighted_polynomial_table: bfloat16 [512, 320, 641], P('band'), may hold values from -0.25 to 0.25
- wavenumber_to_mode_degree: int32 [320], replicated, may hold values from 0 to 319, each once
Outputs:
- smoothed: bfloat16 [8, 2, 512, 4096], P('lev', None, 'band')
- spectral: float32 [8, 2, 2, 320, 641], P('lev', None, None, 'band')
Inputs may be any that keep to these rules, and one draw needn't show every extreme that they name: wavenumber_to_mode_degree holds every pair row 0 to 319 once; pair row p holds wavenumbers p and 639 - p.
All inputs are finite; a program needn't handle non-finite values.
Results may differ from a plain program's by a relative error of at most 0.009.
Values may be sent and summed in bfloat16 or wider, within the bound.
No kernel may reach another device: no remote copies, remote signals or barrier semaphores. Data moves between devices by JAX's collectives and lax.ppermute only.
A program may use at most 128 MiB of HBM per device.

v0:
```python
import math

import jax
import jax.numpy as jnp
from jax import lax
from jax.sharding import PartitionSpec as P

MERIDIAN_STEPS = 1024
K = 640


def padded(cells, sides, width):
    for axis, dim in sides:
        count = lax.axis_size(axis)
        ends = count - 1
        head = lax.slice_in_dim(cells, 0, width, axis=dim)
        tail = lax.slice_in_dim(cells, cells.shape[dim] - width, cells.shape[dim], axis=dim)
        cells = jnp.concatenate(
            [
                lax.ppermute(tail, axis, [(i, (i + 1) % count) for i in range(ends)]),
                cells,
                lax.ppermute(head, axis, [((i + 1) % count, i) for i in range(ends)]),
            ],
            axis=dim,
        )
    return cells


def carried_in(shard, axis, join, neutral):
    count = lax.axis_size(axis)
    place = lax.axis_index(axis)
    ahead = count - 1 - place
    gathered = lax.all_gather(shard.astype(jnp.bfloat16), axis)
    state = jnp.zeros_like(shard) + jnp.asarray(neutral, shard.dtype)

    def one(turn, state):
        source = count - 1 - turn
        return join(state, lax.dynamic_index_in_dim(gathered, source, 0, False).astype(shard.dtype))

    return lax.fori_loop(0, ahead, one, state)


def pair_terms(products, pair_index, columns):
    count_pairs = products.shape[0]
    products = products.reshape(count_pairs, 4, products.shape[1] // 4, columns)
    column_ids = jnp.arange(columns, dtype=jnp.int32)[None, :]
    pair_ids = pair_index[:, None]
    first_part = column_ids < columns - 1 - pair_ids
    parity = jnp.where(first_part, column_ids % 2, (column_ids + pair_ids) % 2)
    signs = (1 - 2 * parity).astype(products.dtype)[:, None, :]
    first_part = first_part[:, None, :]
    return jnp.where(
        first_part, products[:, 0] + signs * products[:, 1], products[:, 2] + signs * products[:, 3]
    )


def batched_product(coeff_rows, table_rows):
    return lax.dot_general(
        coeff_rows, table_rows, (((2,), (0,)), ((0,), (1,))), preferred_element_type=jnp.float32
    )


def add_terms(earlier, later):
    return earlier + later


def on_device(
    air_heat_state,
    mixing_coefficient,
    layer_depth_factor,
    weighted_polynomial_table,
    wavenumber_to_mode_degree,
):
    levels_held_locally, hemisphere_pair, latitude_row_count, longitude_cell_count = (
        air_heat_state.shape
    )
    current_band_index = lax.axis_index("band")
    number_of_bands = lax.axis_size("band")
    half_k = K // 2
    slots = half_k // number_of_bands
    padded_with_nulls = padded(air_heat_state, (("band", 2),), 1)
    physical_space_values = air_heat_state.astype(jnp.float32)
    kappa_field = mixing_coefficient.astype(jnp.float32)
    global_rows = (
        current_band_index * latitude_row_count + jnp.arange(latitude_row_count, dtype=jnp.int32)
    ).astype(jnp.float32)
    centre = jnp.sin((global_rows + 0.5) * (math.pi / MERIDIAN_STEPS))[:, None]
    upper_face = jnp.sin((global_rows + 1.0) * (math.pi / MERIDIAN_STEPS))[:, None]
    lower_face = jnp.sin(global_rows * (math.pi / MERIDIAN_STEPS))[:, None]
    eastward = jnp.roll(physical_space_values, -1, axis=3)
    westward = jnp.roll(physical_space_values, 1, axis=3)
    poleward = padded_with_nulls[:, :, :latitude_row_count].astype(jnp.float32)
    beyond = jnp.where(
        current_band_index == number_of_bands - 1,
        air_heat_state[:, ::-1, -1:],
        padded_with_nulls[:, :, latitude_row_count + 1 :],
    )
    equatorward = jnp.concatenate(
        [padded_with_nulls[:, :, 2 : latitude_row_count + 1], beyond], axis=2
    ).astype(jnp.float32)
    meridional = (
        upper_face * (equatorward - physical_space_values)
        - lower_face * (physical_space_values - poleward)
    ) / centre
    smoothed = (
        physical_space_values
        + kappa_field[None] * (eastward - 2.0 * physical_space_values + westward + meridional)
    ).astype(jnp.bfloat16)
    weighted = layer_depth_factor[:, None, None, None] * smoothed.astype(jnp.float32)
    local_total = jnp.sum(weighted, axis=0)
    below = carried_in(local_total, "lev", add_terms, jnp.zeros_like(local_total))
    from_ground = below[None] + jnp.cumsum(weighted[::-1], axis=0)[::-1]
    geopotential = (from_ground - 0.5 * weighted).astype(jnp.bfloat16)
    grid = jnp.stack([smoothed, geopotential], axis=1)
    flat = grid.reshape(-1, longitude_cell_count)
    scale_factor = 1.0 / math.sqrt(longitude_cell_count)

    def transform(block_start):
        frequency = block_start + jnp.arange(128, dtype=jnp.int32)
        phase = (
            jnp.arange(longitude_cell_count, dtype=jnp.int32)[:, None]
            * frequency[None, :]
            % longitude_cell_count
        )
        angle = phase.astype(jnp.float32) * (2.0 * math.pi / longitude_cell_count)
        table = (jnp.concatenate([jnp.cos(angle), -jnp.sin(angle)], axis=1) * scale_factor).astype(
            jnp.bfloat16
        )
        return jnp.dot(flat, table, preferred_element_type=jnp.float32).astype(jnp.bfloat16)

    blocks = lax.map(transform, jnp.arange(0, K, 128, dtype=jnp.int32))
    real_part = jnp.transpose(blocks[:, :, :128], (1, 0, 2)).reshape(
        levels_held_locally, 2, 2, latitude_row_count, K
    )
    imag_part = jnp.transpose(blocks[:, :, 128:], (1, 0, 2)).reshape(
        levels_held_locally, 2, 2, latitude_row_count, K
    )
    fourier = jnp.stack([real_part, imag_part], axis=2)
    channels = levels_held_locally * 4
    north = fourier[:, :, :, 0].reshape(channels, latitude_row_count, K)
    south = fourier[:, :, :, 1].reshape(channels, latitude_row_count, K)
    stacked = jnp.stack(
        [
            north[..., :half_k],
            south[..., :half_k],
            north[..., ::-1][..., :half_k],
            south[..., ::-1][..., :half_k],
        ],
        axis=0,
    )
    arranged = jnp.transpose(stacked, (3, 0, 1, 2)).reshape(
        half_k, 4 * channels, latitude_row_count
    )
    own_pairs = lax.dynamic_slice_in_dim(
        wavenumber_to_mode_degree, current_band_index * slots, slots
    )

    def whole_block(block_start):
        coeff_block = lax.dynamic_slice_in_dim(arranged, block_start, 32, 0)
        table_block = lax.dynamic_slice_in_dim(weighted_polynomial_table, block_start, 32, 1)
        products = batched_product(coeff_block, table_block)
        return pair_terms(products, block_start + jnp.arange(32, dtype=jnp.int32), K + 1)

    partial_sums = lax.map(whole_block, jnp.arange(0, half_k, 32, dtype=jnp.int32)).reshape(
        half_k, channels, K + 1
    )
    summed = lax.psum(partial_sums, "band")
    mine = jnp.take(summed, own_pairs, axis=0)
    spectral = jnp.transpose(mine.reshape(slots, levels_held_locally, 2, 2, K + 1), (1, 2, 3, 0, 4))
    return (smoothed, spectral)


def solution(mesh):
    placed = (
        P("lev", None, "band", None),
        P(None, "band", None),
        P("lev"),
        P("band", None, None),
        P(),
    )
    return jax.shard_map(
        on_device,
        mesh=mesh,
        in_specs=placed,
        out_specs=(P("lev", None, "band", None), P("lev", None, None, "band", None)),
        check_vma=False,
    )
```

profile of v0, /device:TPU:0, one launch (start us, length us, event | category | flops | bytes accessed | tf_op | source)
XLA Modules:
  0.0 544.2 jit_solution(9794864033026689576)
XLA Ops:
  10.6 3.7 collective-permute-start.1
  14.4 6.5 %fusion.51 = (f32[4,2,32,4095]{3,2,1,0:T(8,128)}, f32[4,2,32,4095]{3,2,1,0:T(8,128)}) fusion(bf16[4,2,32,4096]{3,2,1,0:T(8,128)(2,1)} %param.11), kind=kLoop, calls=%fused_computation.87 | loop fusion | bytes 16773120 | tf_op jit(solution)/shard_map/jit(_roll_static)/slice | solution.py:90
  26.2 7.4 %fusion.49 = (bf16[2,32,4096]{2,1,0:T(8,128)(2,1)}, bf16[4,2,32,4096]{3,2,1,0:T(8,128)(2,1)S(1)}) fusion(f32[4]{0:T(128)S(1)} %copy-done.6, f32[32]{0:T(128)S(1)} %get-tuple-element.248, bf16[4,2,32,4096]{3,2,1,0:T(8,128)(2,1)S(1)} %copy-done, bf16[4,2,1,4096]{3,2,1,0:T(2,128)(2,1)} %collective-permute-done.1, f32[32]{0:T(128)S(1)} %get-tuple-element.249, ...), kind=kLoop, calls=%fused_computation.86 | loop fusion | flops 28049408 | bytes 16318864 | tf_op jit(solution)/shard_map/reduce_sum | solution.py:110
  34.9 2.5 convert_multiply_fusion
  37.5 4.6 rev.12
  42.2 4.4 fusion.55
  46.6 19.7 %all-gather.3.cloned.1.call-done = bf16[4,32,4096]{2,1,0:T(8,128)(2,1)} async-done(((bf16[2,32,4096]{2,1,0:T(8,128)(2,1)}), bf16[4,32,4096]{2,1,0:T(8,128)(2,1)}) %all-gather.3.cloned.1.call-update) | async-done | bytes 1048592 | tf_op jit(solution)/shard_map/all_gather | solution.py:33
  68.1 3.0 fusion.48
  71.2 2.3 pad_maximum_fusion
  73.5 55.6 %while.37 = (s32[]{:T(128)}, bf16[5,512,256]{1,2,0:T(8,128)(2,1)S(1)}, s32[5]{0:T(128)S(1)}, bf16[512,4096]{1,0:T(8,128)(2,1)}, s32[]{:T(128)}) while((s32[]{:T(128)}, bf16[5,512,256]{1,2,0:T(8,128)(2,1)S(1)}, s32[5]{0:T(128)S(1)}, bf16[512,4096]{1,0:T(8,128)(2,1)}, s32[]{:T(128)}) %tuple.110), condition=%wide.region_5.6_spmd, body=%wide.region_4.5_spmd.sunk | while | flops 1084883072 | bytes 29623404 | solution.py:131
  75.0 8.2 %fusion.69 = (f32[4096,128]{1,0:T(8,128)S(1)}, f32[4096,128]{1,0:T(8,128)S(1)}) fusion(s32[128]{0:T(128)S(1)} %iota_add_fusion.5), kind=kLoop, calls=%fused_computation.19.clone.1 | loop fusion | flops 7864320 | bytes 4194816 | tf_op jit(solution)/shard_map/while/body/eval_jaxpr/cos | solution.py:126
  86.2 8.2 %fusion.69 = (f32[4096,128]{1,0:T(8,128)S(1)}, f32[4096,128]{1,0:T(8,128)S(1)}) fusion(s32[128]{0:T(128)S(1)} %iota_add_fusion.5), kind=kLoop, calls=%fused_computation.19.clone.1 | loop fusion | flops 7864320 | bytes 4194816 | tf_op jit(solution)/shard_map/while/body/eval_jaxpr/cos | solution.py:126
  97.3 8.2 %fusion.69 = (f32[4096,128]{1,0:T(8,128)S(1)}, f32[4096,128]{1,0:T(8,128)S(1)}) fusion(s32[128]{0:T(128)S(1)} %iota_add_fusion.5), kind=kLoop, calls=%fused_computation.19.clone.1 | loop fusion | flops 7864320 | bytes 4194816 | tf_op jit(solution)/shard_map/while/body/eval_jaxpr/cos | solution.py:126
  108.4 8.2 %fusion.69 = (f32[4096,128]{1,0:T(8,128)S(1)}, f32[4096,128]{1,0:T(8,128)S(1)}) fusion(s32[128]{0:T(128)S(1)} %iota_add_fusion.5), kind=kLoop, calls=%fused_computation.19.clone.1 | loop fusion | flops 7864320 | bytes 4194816 | tf_op jit(solution)/shard_map/while/body/eval_jaxpr/cos | solution.py:126
  119.6 8.2 %fusion.69 = (f32[4096,128]{1,0:T(8,128)S(1)}, f32[4096,128]{1,0:T(8,128)S(1)}) fusion(s32[128]{0:T(128)S(1)} %iota_add_fusion.5), kind=kLoop, calls=%fused_computation.19.clone.1 | loop fusion | flops 7864320 | bytes 4194816 | tf_op jit(solution)/shard_map/while/body/eval_jaxpr/cos | solution.py:126
  139.4 5.8 %copy.37 = bf16[320,64,32]{1,2,0:T(8,128)(2,1)} copy(bf16[320,64,32]{0,2,1:T(8,128)(2,1)S(1)} %bitcast.101) | data formatting | bytes 2621440 | tf_op jit(solution)/shard_map/while | solution.py:164
  145.2 103.1 %while.38 = (s32[]{:T(128)}, f32[10,32,16,641]{3,2,1,0:T(8,128)}, s32[10]{0:T(128)S(1)}, bf16[320,64,32]{1,2,0:T(8,128)(2,1)}, bf16[32,320,641]{2,1,0:T(8,128)(2,1)}, /*index=5*/s32[]{:T(128)}, s32[]{:T(128)}, s32[]{:T(128)}) while((s32[]{:T(128)}, f32[10,32,16,641]{3,2,1,0:T(8,128)}, s32[10]{0:T(128)S(1)}, bf16[320,64,32]{1,2,0:T(8,128)(2,1)}, ...), condition=%wide.region_7.8_spmd, body=%wide.region_6.7_spmd.sunk | while | flops 86031240 | bytes 16486999 | solution.py:164
  150.1 2.7 fusion.73
  158.1 2.3 constant_dynamic-slice_fusion.2
  160.4 2.7 fusion.73
  168.4 2.3 constant_dynamic-slice_fusion.2
  170.7 2.7 fusion.73
  181.0 2.7 fusion.73
  191.3 2.7 fusion.73
  199.3 2.3 constant_dynamic-slice_fusion.2
  201.6 2.7 fusion.73
  212.0 2.7 fusion.73
  222.3 2.7 fusion.73
  232.7 2.7 fusion.73
  242.9 2.7 fusion.73
  249.1 279.7 %all-reduce.2.cloned.1.call-done = f32[320,16,641]{2,1,0:T(8,128)} async-done(((f32[320,16,641]{2,1,0:T(8,128)}), f32[320,16,641]{2,1,0:T(8,128)}) %all-reduce.2.cloned.1.call-update) | async-done | bytes 13127696 | tf_op jit(solution)/shard_map/psum | solution.py:167
  528.8 6.1 %gather_fusion = f32[20,16,641]{2,1,0:T(8,128)S(1)} fusion(f32[320,16,641]{2,1,0:T(8,128)} %all-reduce.2.cloned.1.call-done, s32[1024]{0:T(1024)S(1)} %pad_clamp_fusion), kind=kCustom, calls=%fused_computation | custom fusion | bytes 1641040 | tf_op jit(solution)/shard_map/jit(_take)/gather | solution.py:168
  (151 shorter events, 90.7 us)
Async XLA Ops:
  7.2 59.1 %all-gather.3.cloned.1.call-start = ((), (), s32[]{:S(2)}) async-start(), calls=%async_computation.1 | async-start | bytes 1572864 | tf_op jit(solution)/shard_map/all_gather | solution.py:33
  9.3 15.7 %collective-permute-start = (bf16[4,2,1,4096]{3,2,1,0:T(2,128)(2,1)}, bf16[4,2,1,4096]{3,2,1,0:T(2,128)(2,1)}, u32[]{:S(2)}, u32[]{:S(2)}) collective-permute-start(bf16[4,2,1,4096]{3,2,1,0:T(2,128)(2,1)} %get-tuple-element.238), channel_id=1, source_target_pairs={{2,0},{4,2},{6,4},{8,6},{10,8},{12,10},{14,12},{16,14},{18,16},{20... | collective-permute-start | bytes 196616 | tf_op jit(solution)/shard_map/ppermute | solution.py:22
  10.6 15.6 %collective-permute-start.1 = (bf16[4,2,1,4096]{3,2,1,0:T(2,128)(2,1)S(1)}, bf16[4,2,1,4096]{3,2,1,0:T(2,128)(2,1)}, u32[]{:S(2)}, u32[]{:S(2)}) collective-permute-start(bf16[4,2,1,4096]{3,2,1,0:T(2,128)(2,1)S(1)} %get-tuple-element.239), channel_id=1, source_target_pairs={{0,2},{2,4},{4,6},{6,8},{8,10},{10,12},{12,14},{14,16},{16,18},{18... | collective-permute-start | bytes 196616 | tf_op jit(solution)/shard_map/ppermute | solution.py:20
  14.4 6.5 %copy-start = (bf16[4,2,32,4096]{3,2,1,0:T(8,128)(2,1)S(1)}, bf16[4,2,32,4096]{3,2,1,0:T(8,128)(2,1)}, u32[]{:S(2)}) copy-start(bf16[4,2,32,4096]{3,2,1,0:T(8,128)(2,1)} %param.11) | copy-start | bytes 6291460
  21.0 5.2 copy-start.6
  33.6 1.3 copy-start.1
  42.1 486.7 %all-reduce.2.cloned.1.call-start = ((), (), s32[]{:S(2)}) async-start(), calls=%async_computation | async-start | bytes 31457280 | tf_op jit(solution)/shard_map/psum | solution.py:167
  66.3 1.8 copy-start.2
  71.1 2.3 copy-start.4
  71.2 2.3 copy-start.8
  73.5 9.8 %copy-start.3 = (bf16[512,4096]{1,0:T(8,128)(2,1)S(1)}, bf16[512,4096]{1,0:T(8,128)(2,1)}, u32[]{:S(2)}) copy-start(bf16[512,4096]{1,0:T(8,128)(2,1)} %get-tuple-element.374) | copy-start | bytes 12582916 | tf_op jit(solution)/shard_map/while
  84.6 9.8 %copy-start.3 = (bf16[512,4096]{1,0:T(8,128)(2,1)S(1)}, bf16[512,4096]{1,0:T(8,128)(2,1)}, u32[]{:S(2)}) copy-start(bf16[512,4096]{1,0:T(8,128)(2,1)} %get-tuple-element.374) | copy-start | bytes 12582916 | tf_op jit(solution)/shard_map/while
  95.7 9.8 %copy-start.3 = (bf16[512,4096]{1,0:T(8,128)(2,1)S(1)}, bf16[512,4096]{1,0:T(8,128)(2,1)}, u32[]{:S(2)}) copy-start(bf16[512,4096]{1,0:T(8,128)(2,1)} %get-tuple-element.374) | copy-start | bytes 12582916 | tf_op jit(solution)/shard_map/while
  106.9 9.8 %copy-start.3 = (bf16[512,4096]{1,0:T(8,128)(2,1)S(1)}, bf16[512,4096]{1,0:T(8,128)(2,1)}, u32[]{:S(2)}) copy-start(bf16[512,4096]{1,0:T(8,128)(2,1)} %get-tuple-element.374) | copy-start | bytes 12582916 | tf_op jit(solution)/shard_map/while
  118.0 9.8 %copy-start.3 = (bf16[512,4096]{1,0:T(8,128)(2,1)S(1)}, bf16[512,4096]{1,0:T(8,128)(2,1)}, u32[]{:S(2)}) copy-start(bf16[512,4096]{1,0:T(8,128)(2,1)} %get-tuple-element.374) | copy-start | bytes 12582916 | tf_op jit(solution)/shard_map/while
  129.1 1.1 copy-start.5
  139.4 5.8 %copy-start.7 = (s32[10]{0:T(128)S(1)}, s32[10]{0:T(128)}, u32[]{:S(2)}) copy-start(s32[10]{0:T(128)} %iota_multiply_fusion.1) | copy-start | bytes 124
Sparse Core Ops, SparseCore 0:
  42.2 23.9 all-gather.2
  248.5 280.2 all-reduce.1
where the time goes:
time: 546 us; the launch traced here: 544 us
  waiting for transfers between devices  299 us (55%)
  other arithmetic  100 us (18%)
  local copies, waits for them, and re-layouts  72.1 us (13%)
  matrix products  33.2 us (6%)
  loops' own time  20.1 us (4%)
  between operations  14.3 us (3%)
    psum x1, waiting for transfers between devices, on_device(): summed = lax.psum(partial_sums, 'band')  280 us
    cos x5, other arithmetic, transform(): jnp.cos(angle)  41.2 us
    dot_general x10, matrix products, batched_product(): lax.dot_general(coeff_rows, table_rows, (((2,), (0,)), ((0,), (1,))), pre...  26.6 us
    dynamic_slice x10, local copies, waits for them, and re-layouts, whole_block(): lax.dynamic_slice_in_dim(weighted_polynomial_table, block_start, 32, 1)  22.9 us
    another operation x1, loops' own time, on_device(): lax.map(whole_block, jnp.arange(0, half_k, 32, dtype=jnp.int32))  19.8 us
    all_gather x1, waiting for transfers between devices, carried_in(): gathered = lax.all_gather(shard.astype(jnp.bfloat16), axis)  19.7 us
    dynamic_update_slice x10, other arithmetic, on_device(): lax.map(whole_block, jnp.arange(0, half_k, 32, dtype=jnp.int32))  19.3 us
  transfers between devices with their start and end apart: 4, of which 2 were waited for; matrix products, arithmetic and copies ran while one was open for 3% of the time, Pallas kernels for 0%

commit v1 on v0

v1 whole, which is shorter than its diff:
```python
import functools
import math

import jax
import jax.numpy as jnp
import numpy as np
from jax import lax
from jax.experimental import pallas as pl
from jax.experimental.pallas import tpu as pltpu
from jax.sharding import PartitionSpec as P

GROUP = 8
LANES = 128


def edge_kernel(first_ref, last_ref, head_ref, tail_ref):
    head_ref[...] = first_ref[:, :, 0, :]
    tail_ref[...] = last_ref[:, :, last_ref.shape[2] - 1, :]


def edges(air):
    levels, _, rows, lon = air.shape
    tile = min(8, rows)
    return pl.pallas_call(
        edge_kernel,
        grid=(1,),
        in_specs=[
            pl.BlockSpec((levels, 2, tile, lon), lambda i: (0, 0, 0, 0)),
            pl.BlockSpec((levels, 2, tile, lon), lambda i: (0, 0, rows // tile - 1, 0)),
        ],
        out_specs=[pl.BlockSpec((levels, 2, lon), lambda i: (0, 0, 0))] * 2,
        out_shape=[jax.ShapeDtypeStruct((levels, 2, lon), air.dtype)] * 2,
        name="edges",
    )(air, air)


def wave_kernel(base_cos, base_sin, step_cos, step_sin, out_ref):
    cos, sin = base_cos[0], base_sin[0]
    turn_cos, turn_sin = step_cos[0], step_sin[0]
    lanes = cos.shape[-1]
    for block in range(out_ref.shape[-1] // lanes):
        at = slice(block * lanes, (block + 1) * lanes)
        out_ref[0, 0, :, at] = cos.astype(out_ref.dtype)
        out_ref[0, 1, :, at] = sin.astype(out_ref.dtype)
        cos, sin = cos * turn_cos - sin * turn_sin, sin * turn_cos + cos * turn_sin


def wave_table(lon, top):
    half, count, lanes = lon // 2, top // 4, 128
    index = np.arange(count)
    base, turn = [], []
    for which in range(2):
        for parity in range(2):
            pair = 2 * index + parity
            wave = pair if which == 0 else top - 1 - pair
            phase = wave[:, None] * np.arange(lanes)[None, :] % lon
            base.append(phase * (2.0 * math.pi / lon))
            phase = np.broadcast_to(wave[:, None] * lanes % lon, phase.shape)
            turn.append(phase * (2.0 * math.pi / lon))
    base, turn = np.stack(base), np.stack(turn)
    scale = 1.0 / math.sqrt(lon)
    tables = [
        jnp.asarray(table, jnp.float32)
        for table in (np.cos(base) * scale, -np.sin(base) * scale, np.cos(turn), -np.sin(turn))
    ]
    spec = pl.BlockSpec((1, count // 2, lanes), lambda i, j: (i, j, 0))
    return pl.pallas_call(
        wave_kernel,
        grid=(4, 2),
        in_specs=[spec] * 4,
        out_specs=pl.BlockSpec((1, 2, count // 2, half), lambda i, j: (i, 0, j, 0)),
        out_shape=jax.ShapeDtypeStruct((4, 2, count, half), jnp.bfloat16),
        cost_estimate=pl.CostEstimate(
            flops=4 * 2 * count * half * 3, bytes_accessed=4 * 2 * count * half * 2, transcendentals=0
        ),
        name="waves",
    )(*tables)


def smooth_kernel(
    last_ref, air_ref, kappa_ref, above_ref, below_ref, up_ref, down_ref, out_ref, fold_ref, padded
):
    rows, lon = air_ref.shape[2:]
    half = lon // 2
    is_last = last_ref[0] == 1
    for side in range(2):
        padded[side, 8 : 8 + rows, :] = air_ref[0, side].astype(jnp.float32)
    for side in range(2):
        padded[side, 7:8, :] = above_ref[0, side : side + 1, :].astype(jnp.float32)
        mirrored = padded[1 - side, 7 + rows : 8 + rows, :]
        padded[side, 8 + rows : 9 + rows, :] = jnp.where(
            is_last, mirrored, below_ref[0, side : side + 1, :].astype(jnp.float32)
        )
    tile = min(16, rows)
    for start in range(0, rows, tile):
        at = slice(start, start + tile)
        up, down = up_ref[at, :], down_ref[at, :]
        both = []
        for side in range(2):
            u = padded[side, 8 + start : 8 + start + tile, :]
            poleward = padded[side, 7 + start : 7 + start + tile, :]
            equatorward = padded[side, 9 + start : 9 + start + tile, :]
            east = pltpu.roll(u, lon - 1, 1)
            west = pltpu.roll(u, 1, 1)
            change = east - 2.0 * u + west + (up * (equatorward - u) - down * (u - poleward))
            value = (u + kappa_ref[side, at, :].astype(jnp.float32) * change).astype(jnp.bfloat16)
            out_ref[0, side, at, :] = value
            both.append(value.astype(jnp.float32))
        for sign, mixed in enumerate((both[0] + both[1], both[0] - both[1])):
            near, far = mixed[:, :half], mixed[:, half:]
            fold_ref[0, sign, 0, at, :] = (near + far).astype(jnp.bfloat16)
            fold_ref[1, sign, 0, at, :] = (near - far).astype(jnp.bfloat16)


def smooth(air, kappa, above, below, up, down, is_last):
    levels, _, rows, lon = air.shape
    whole = lambda i: (0, 0)
    return pl.pallas_call(
        smooth_kernel,
        grid=(levels,),
        in_specs=[
            pl.BlockSpec(memory_space=pltpu.SMEM),
            pl.BlockSpec((1, 2, rows, lon), lambda i: (i, 0, 0, 0)),
            pl.BlockSpec((2, rows, lon), lambda i: (0, 0, 0)),
            pl.BlockSpec((1, 2, lon), lambda i: (i, 0, 0)),
            pl.BlockSpec((1, 2, lon), lambda i: (i, 0, 0)),
            pl.BlockSpec((rows, 1), whole),
            pl.BlockSpec((rows, 1), whole),
        ],
        out_specs=[
            pl.BlockSpec((1, 2, rows, lon), lambda i: (i, 0, 0, 0)),
            pl.BlockSpec((2, 2, 1, rows, lon // 2), lambda i: (0, 0, i, 0, 0)),
        ],
        out_shape=[
            jax.ShapeDtypeStruct(air.shape, jnp.bfloat16),
            jax.ShapeDtypeStruct((2, 2, levels, rows, lon // 2), jnp.bfloat16),
        ],
        scratch_shapes=[pltpu.VMEM((2, rows + 16, lon), jnp.float32)],
        cost_estimate=pl.CostEstimate(
            flops=20 * air.size, bytes_accessed=7 * air.size, transcendentals=0
        ),
        name="smooth",
    )(is_last, air, kappa, above, below, up, down)


def fourier_kernel(rows, wave_ref, fold_ref, out_ref, lines):
    which = pl.program_id(0)
    count = wave_ref.shape[2]
    width = fold_ref.shape[1]
    tiles = lines.shape[0]
    for parity in range(2):
        field = fold_ref[(which + parity) % 2]
        if width < LANES:
            spare = jnp.zeros((LANES - width, field.shape[1]), field.dtype)
            field = jnp.concatenate([field, spare], axis=0)
        waves = wave_ref[parity].reshape(2 * count, wave_ref.shape[3])
        found = lax.dot_general(
            waves, field, (((1,), (1,)), ((), ())), preferred_element_type=jnp.float32
        )
        for part in range(2):
            for tile in range(tiles):
                lines[tile, part, pl.ds(parity, count, stride=2), :] = found[
                    part * count : (part + 1) * count, tile * LANES : (tile + 1) * LANES
                ]
    values = [
        jnp.concatenate([lines[tile, part] for tile in range(tiles)], axis=1).astype(jnp.bfloat16)
        for part in range(2)
    ]
    wide = GROUP * rows
    source = lax.broadcasted_iota(jnp.int32, (tiles * LANES, wide), 0)
    target = lax.broadcasted_iota(jnp.int32, (tiles * LANES, wide), 1)
    own = lax.broadcasted_iota(jnp.int32, (1, GROUP, wide), 1) == (
        lax.broadcasted_iota(jnp.int32, (1, GROUP, wide), 2) & (GROUP - 1)
    )
    for block in range(width // rows):
        spread = jnp.where(source == block * rows + (target >> 3), 1.0, 0.0).astype(jnp.bfloat16)
        sides = []
        for part in range(2):
            copied = jnp.dot(values[part], spread, preferred_element_type=jnp.float32)
            sides.append(jnp.where(own, copied.reshape(-1, GROUP, wide), 0.0))
        out_ref[:, 0, block * 2 * GROUP : (block + 1) * 2 * GROUP, :] = jnp.concatenate(
            sides, axis=1
        ).astype(jnp.bfloat16)


def fourier_blocks(waves, folds, rows):
    _, _, count, half = waves.shape
    width = folds.shape[1]
    pairs = 2 * count
    blocks = width // rows
    wide = GROUP * rows
    return pl.pallas_call(
        functools.partial(fourier_kernel, rows),
        grid=(2,),
        in_specs=[
            pl.BlockSpec((2, 2, count, half), lambda i: (i, 0, 0, 0)),
            pl.BlockSpec((2, width, half), lambda i: (0, 0, 0)),
        ],
        out_specs=pl.BlockSpec((pairs // GROUP, 1, blocks * 2 * GROUP, wide), lambda i: (0, i, 0, 0)),
        out_shape=jax.ShapeDtypeStruct((pairs // GROUP, 2, blocks * 2 * GROUP, wide), jnp.bfloat16),
        scratch_shapes=[pltpu.VMEM((pl.cdiv(width, LANES), 2, pairs, LANES), jnp.float32)],
        compiler_params=pltpu.CompilerParams(vmem_limit_bytes=60 << 20),
        cost_estimate=pl.CostEstimate(
            flops=2 * 8 * count * half * width,
            bytes_accessed=2 * (waves.size + folds.size),
            transcendentals=0,
        ),
        name="fourier",
    )(waves, folds)


def legendre_kernel(place_ref, block_ref, table_ref, out_ref, turned):
    step = pl.program_id(0)
    rows, pairs, columns = table_ref.shape
    groups = pairs // GROUP
    channels = out_ref.shape[1]
    for group in range(groups):
        table = table_ref[:, group * GROUP : (group + 1) * GROUP, :].reshape(rows * GROUP, columns)
        left = block_ref[group].reshape(4 * channels * GROUP, rows * GROUP)
        sums = jnp.dot(left, table, preferred_element_type=jnp.float32)
        sums = sums.reshape(2, 2, channels, GROUP, columns)
        first_pair = (step * groups + group) * GROUP
        pair = first_pair + lax.broadcasted_iota(jnp.int32, (GROUP, columns), 0)
        column = lax.broadcasted_iota(jnp.int32, (GROUP, columns), 1)
        first = column < columns - 1 - pair
        odd = jnp.where(first, column, column - (columns - 1) + pair) & 1
        even = (odd == 0)[None]
        chosen = jnp.where(
            first[None],
            jnp.where(even, sums[0, 0], sums[0, 1]),
            jnp.where(even, sums[1, 0], sums[1, 1]),
        )
        chosen = chosen.reshape(channels * GROUP, columns)
        for tile in range(turned.shape[0]):
            start, end = tile * LANES, min(columns, (tile + 1) * LANES)
            turned[tile, :, : end - start] = chosen[:, start:end]
        for member in range(GROUP):
            place = place_ref[first_pair + member]
            for tile in range(turned.shape[0]):
                start, end = tile * LANES, min(columns, (tile + 1) * LANES)
                value = turned[tile, pl.ds(member, channels, stride=GROUP), :]
                out_ref[place, :, start:end] = value[:, : end - start].astype(out_ref.dtype)


def legendre(places, blocks, table):
    rows, half_k, columns = table.shape
    channels = blocks.shape[1] * blocks.shape[2] // (4 * GROUP)
    pairs = 2 * GROUP
    groups = pairs // GROUP
    return pl.pallas_call(
        legendre_kernel,
        grid_spec=pltpu.PrefetchScalarGridSpec(
            num_scalar_prefetch=1,
            grid=(half_k // pairs,),
            in_specs=[
                pl.BlockSpec((groups, *blocks.shape[1:]), lambda i, s: (i, 0, 0, 0)),
                pl.BlockSpec((rows, pairs, columns), lambda i, s: (0, i, 0)),
            ],
            out_specs=pl.BlockSpec((half_k, channels, columns), lambda i, s: (0, 0, 0)),
            scratch_shapes=[pltpu.VMEM((pl.cdiv(columns, LANES), channels * GROUP, LANES), jnp.float32)],
        ),
        out_shape=jax.ShapeDtypeStruct((half_k, channels, columns), jnp.bfloat16),
        compiler_params=pltpu.CompilerParams(vmem_limit_bytes=60 << 20),
        cost_estimate=pl.CostEstimate(
            flops=2 * blocks.size * columns,
            bytes_accessed=2 * (blocks.size + table.size),
            transcendentals=0,
        ),
        name="legendre",
    )(places, blocks, table)


def reversed_bits(value, bits):
    result = jnp.zeros_like(value)
    for bit in range(bits):
        result = result * 2 + ((value >> bit) & 1)
    return result


def on_device(air, kappa, depth, table, mode_degree):
    levels, _, rows, lon = air.shape
    half_k, columns = table.shape[1:]
    band = lax.axis_index("band")
    bands = lax.axis_size("band")
    bits = bands.bit_length() - 1
    slots = half_k // bands
    steps = 2 * rows * bands

    head, tail = edges(air)
    below = lax.ppermute(head, "band", [(i + 1, i) for i in range(bands - 1)])
    above = lax.ppermute(tail, "band", [(i, i + 1) for i in range(bands - 1)])

    waves = wave_table(lon, columns - 1)
    row = (band * rows + jnp.arange(rows, dtype=jnp.int32)).astype(jnp.float32)[:, None]
    centre = jnp.sin((row + 0.5) * (math.pi / steps))
    up = jnp.sin((row + 1.0) * (math.pi / steps)) / centre
    down = jnp.sin(row * (math.pi / steps)) / centre
    is_last = (band == bands - 1).astype(jnp.int32)[None]
    slot = jnp.arange(half_k, dtype=jnp.int32)
    place = reversed_bits((slot // slots) ^ band, bits) * slots + slot % slots
    places = jnp.sum(
        jnp.where(mode_degree[None, :] == slot[:, None], place[None, :], 0), axis=1, dtype=jnp.int32
    )

    smoothed, folds = smooth(air, kappa, above, below, up, down, is_last)
    blocks = fourier_blocks(waves, folds.reshape(2, 2 * levels * rows, lon // 2), rows)
    held = [legendre(places, blocks, table)]
    count = half_k
    for bit in range(bits):
        count //= 2
        outgoing = sum(part[count : 2 * count].astype(jnp.float32) for part in held)
        held.append(
            lax.ppermute(
                outgoing.astype(jnp.bfloat16), "band", [(i, i ^ (1 << bit)) for i in range(bands)]
            )
        )
    mine = sum(part[:slots].astype(jnp.float32) for part in held)
    mine = mine.reshape(slots, levels, 2, columns)
    weighted = depth[None, :, None, None] * mine
    levs = lax.axis_size("lev")
    total = jnp.sum(weighted, axis=1)
    lower = jnp.zeros_like(total)
    if levs > 1:
        lower = lax.ppermute(total, "lev", [(i + 1, i) for i in range(levs - 1)])
        reach = 1
        while reach < levs - 1:
            lower = lower + lax.ppermute(lower, "lev", [(i + reach, i) for i in range(levs - reach)])
            reach *= 2
    potential = []
    for level in reversed(range(levels)):
        potential.append(lower + 0.5 * weighted[:, level])
        lower = lower + weighted[:, level]
    fields = jnp.stack([mine, jnp.stack(potential[::-1], axis=1)], axis=2)
    return smoothed, jnp.transpose(fields, (1, 2, 3, 0, 4))


def solution(mesh):
    placed = (
        P("lev", None, "band", None),
        P(None, "band", None),
        P("lev"),
        P("band", None, None),
        P(),
    )
    return jax.shard_map(
        on_device,
        mesh=mesh,
        in_specs=placed,
        out_specs=(P("lev", None, "band", None), P("lev", None, None, "band", None)),
        check_vma=False,
    )
```

time: 546 us -> 120 us (0.22)
  waiting for transfers between devices: 299 us -> 51.5 us
  other arithmetic: 100 us -> 4.5 us
  local copies, waits for them, and re-layouts: 72.1 us -> 3.04 us
  Pallas kernels: 0 us -> 43.1 us
  matrix products: 33.2 us -> 0 us
  loops' own time: 20.1 us -> 0 us
  between operations: 14.3 us -> 0.77 us
  starting transfers between devices: 5.05 us -> 15.9 us
    psum x1 -> x0, waiting for transfers between devices: 280 us -> none  [on_device(): summed = lax.psum(partial_sums, 'band')]
    ppermute x2 -> x7, waiting for transfers between devices: 0.01 us -> 51.5 us  [the longest x4 46.3 us: on_device(): lax.ppermute(outgoing.astype(jnp.bfloat16), 'band', [(i, i ^ 1 << bit) fo...]
    pallas_call x0 -> x5, Pallas kernels: none -> 43.1 us  [the longest x1 20 us: legendre(): pl.pallas_call(legendre_kernel, grid_spec=pltpu.PrefetchScalarGridSpec(nu...]
    cos x5 -> x0, other arithmetic: 41.2 us -> none  [transform(): jnp.cos(angle)]
    dot_general x15 -> x0, matrix products: 33.2 us -> none  [the longest x10 26.6 us: batched_product(): lax.dot_general(coeff_rows, table_rows, (((2,), (0,)), ((0,), (1,))), pre...]
    dynamic_slice x25 -> x0, local copies, waits for them, and re-layouts: 31.7 us -> none  [the longest x10 22.9 us: whole_block(): lax.dynamic_slice_in_dim(weighted_polynomial_table, block_start, 32, 1)]
    another operation x3 -> x0, loops' own time: 20.1 us -> none  [the longest x1 19.8 us: on_device(): lax.map(whole_block, jnp.arange(0, half_k, 32, dtype=jnp.int32))]
    all_gather x1 -> x0, waiting for transfers between devices: 19.7 us -> none  [carried_in(): gathered = lax.all_gather(shard.astype(jnp.bfloat16), axis)]
  transfers between devices with their start and end apart: 4 -> 7, of which waited for: 2 -> 5; matrix products, arithmetic and copies ran while one was open for 3% -> 1% of each run, Pallas kernels for 0% -> 5%
where the time goes in v1:
time: 120 us; the launch traced here: 119 us
  waiting for transfers between devices  51.5 us (43%)
  Pallas kernels  43.1 us (36%)
  starting transfers between devices  15.9 us (13%)
  other arithmetic  4.5 us (4%)
  local copies, waits for them, and re-layouts  3.04 us (3%)
    ppermute x4, waiting for transfers between devices, on_device(): lax.ppermute(outgoing.astype(jnp.bfloat16), 'band', [(i, i ^ 1 << bit) fo...  46.3 us
    pallas_call x1, Pallas kernels, legendre(): pl.pallas_call(legendre_kernel, grid_spec=pltpu.PrefetchScalarGridSpec(nu...  20 us
    ppermute x4, starting transfers between devices, on_device(): lax.ppermute(outgoing.astype(jnp.bfloat16), 'band', [(i, i ^ 1 << bit) fo...  10.9 us
    pallas_call x1, Pallas kernels, fourier_blocks(): pl.pallas_call(functools.partial(fourier_kernel, rows), grid=(2,), in_spe...  7.42 us
    pallas_call x1, Pallas kernels, smooth(): pl.pallas_call(smooth_kernel, grid=(levels,), in_specs=[pl.BlockSpec(memo...  7.33 us
    pallas_call x1, Pallas kernels, wave_table(): pl.pallas_call(wave_kernel, grid=(4, 2), in_specs=[spec] * 4, out_specs=p...  6.23 us
    ppermute x1, waiting for transfers between devices, on_device(): lower = lax.ppermute(total, 'lev', [(i + 1, i) for i in range(levs - 1)])  5.18 us
  transfers between devices with their start and end apart: 7, of which 5 were waited for; matrix products, arithmetic and copies ran while one was open for 1% of the time, Pallas kernels for 5%

profile of v1, /device:TPU:0, one launch (start us, length us, event | category | flops | bytes accessed | tf_op | source)
XLA Modules:
  0.0 118.9 jit_solution(557517067956142437)
XLA Ops:
  0.6 2.2 %edges.1 = (bf16[4,2,4096]{2,1,0:T(2,128)(2,1)}, bf16[4,2,4096]{2,1,0:T(2,128)(2,1)}) custom-call(bf16[4,2,32,4096]{3,2,1,0:T(8,128)(2,1)} %air_ref.1, bf16[4,2,32,4096]{3,2,1,0:T(8,128)(2,1)} %air_ref.1), custom_call_target="tpu_custom_call" | custom-call | tf_op jit(solution)/shard_map/edges/pallas_call | solution.py:24
  2.8 2.4 %collective-permute-start = (bf16[4,2,4096]{2,1,0:T(2,128)(2,1)}, bf16[4,2,4096]{2,1,0:T(2,128)(2,1)S(1)}, u32[]{:S(2)}, u32[]{:S(2)}) collective-permute-start(bf16[4,2,4096]{2,1,0:T(2,128)(2,1)} %get-tuple-element.6), channel_id=1, source_target_pairs={{0,2},{2,4},{4,6},{6,8},{8,10},{10,12},{12,14},{14,16},{16,18},{18... | collective-permute-start | bytes 196616 | tf_op jit(solution)/shard_map/ppermute | solution.py:291
  5.2 1.3 %collective-permute-start.1 = (bf16[4,2,4096]{2,1,0:T(2,128)(2,1)}, bf16[4,2,4096]{2,1,0:T(2,128)(2,1)S(1)}, u32[]{:S(2)}, u32[]{:S(2)}) collective-permute-start(bf16[4,2,4096]{2,1,0:T(2,128)(2,1)} %get-tuple-element.7), channel_id=1, source_target_pairs={{2,0},{4,2},{6,4},{8,6},{10,8},{12,10},{14,12},{16,14},{18,16},{20... | collective-permute-start | bytes 196616 | tf_op jit(solution)/shard_map/ppermute | solution.py:290
  6.5 0.7 select_reduce_fusion.place_ref
  7.2 6.2 %waves.1.wave_ref = bf16[4,2,160,2048]{3,2,1,0:T(8,128)(2,1)} custom-call(f32[4,160,128]{2,1,0:T(8,128)} %constant.55.clone.base_cos, f32[4,160,128]{2,1,0:T(8,128)} %constant.56.clone.base_sin, f32[4,160,128]{2,1,0:T(8,128)} %constant.57.clone.step_cos, f32[4,160,128]{2,1,0:T(8,128)} %constant.58.clone.step_sin), custom_call_target="tpu_custom_call" | custom-call | flops 7864320 | bytes 5242880 | tf_op jit(solution)/shard_map/waves/pallas_call | solution.py:67
  13.4 0.8 sine_divide_fusion
  14.3 0.6 copy-done.1
  14.8 0.0 copy-done.2
  14.9 7.3 %smooth.1 = (bf16[4,2,32,4096]{3,2,1,0:T(8,128)(2,1)}, bf16[2,2,4,32,2048]{4,3,2,1,0:T(8,128)(2,1)}) custom-call(s32[1]{0:T(128)} %bitcast.last_ref, bf16[4,2,32,4096]{3,2,1,0:T(8,128)(2,1)} %air_ref.1, bf16[2,32,4096]{2,1,0:T(8,128)(2,1)} %kappa_ref.1, bf16[4,2,4096]{2,1,0:T(2,128)(2,1)} %copy-done.1, bf16[4,2,4096]{2,1,0:T(2,128)(2,1)} %copy-done.2, ...), custom_call_target="tpu_custom_call" | custom-call | flops 20971520 | bytes 7340032 | tf_op jit(solution)/shard_map/smooth/pallas_call | solution.py:118
  22.2 7.4 %fourier.1.block_ref = bf16[40,2,128,256]{3,2,1,0:T(8,128)(2,1)} custom-call(bf16[4,2,160,2048]{3,2,1,0:T(8,128)(2,1)} %waves.1.wave_ref, bf16[2,256,2048]{2,1,0:T(8,128)(2,1)} %bitcast.48), custom_call_target="tpu_custom_call" | custom-call | flops 1342177280 | bytes 7340032 | tf_op jit(solution)/shard_map/fourier/pallas_call | solution.py:192
  29.6 20.0 %legendre.1 = bf16[320,8,641]{2,1,0:T(8,128)(2,1)} custom-call(s32[320]{0:T(512)} %select_reduce_fusion.place_ref, bf16[40,2,128,256]{3,2,1,0:T(8,128)(2,1)} %fourier.1.block_ref, bf16[32,320,641]{2,1,0:T(8,128)(2,1)} %table_ref.1), custom_call_target="tpu_custom_call" | custom-call | flops 3360686080 | bytes 18370560 | tf_op jit(solution)/shard_map/legendre/pallas_call | solution.py:250
  49.7 1.8 %slice.76 = bf16[160,8,641]{2,1,0:T(8,128)(2,1)S(1)} slice(bf16[320,8,641]{2,1,0:T(8,128)(2,1)} %legendre.1), slice={[160:320], [0:8], [0:641]} | slice | bytes 3281920 | tf_op jit(solution)/shard_map/slice | solution.py:311
  51.5 3.3 %collective-permute-start.2 = (bf16[160,8,641]{2,1,0:T(8,128)(2,1)S(1)}, bf16[160,8,641]{2,1,0:T(8,128)(2,1)S(1)}, u32[]{:S(2)}, u32[]{:S(2)}) collective-permute-start(bf16[160,8,641]{2,1,0:T(8,128)(2,1)S(1)} %slice.76), channel_id=1, source_target_pairs={{0,2},{2,0},{4,6},{6,4},{8,10},{10,8},{12,14},{14,12},{16,18},{18,... | collective-permute-start | bytes 4922888 | tf_op jit(solution)/shard_map/ppermute | solution.py:313
  54.8 3.6 %collective-permute-done.2 = bf16[160,8,641]{2,1,0:T(8,128)(2,1)S(1)} collective-permute-done((bf16[160,8,641]{2,1,0:T(8,128)(2,1)S(1)}, bf16[160,8,641]{2,1,0:T(8,128)(2,1)S(1)}, u32[]{:S(2)}, u32[]{:S(2)}) %collective-permute-start.2) | collective-permute-done | bytes 1640992 | tf_op jit(solution)/shard_map/ppermute | solution.py:313
  58.4 0.3 add_convert_fusion
  58.6 2.1 %collective-permute-start.3 = (bf16[80,8,641]{2,1,0:T(8,128)(2,1)S(1)}, bf16[80,8,641]{2,1,0:T(8,128)(2,1)S(1)}, u32[]{:S(2)}, u32[]{:S(2)}) collective-permute-start(bf16[80,8,641]{2,1,0:T(8,128)(2,1)S(1)} %add_convert_fusion), channel_id=1, source_target_pairs={{0,4},{2,6},{4,0},{6,2},{8,12},{10,14},{12,8},{14,10},{16,20},{18,... | collective-permute-start | bytes 2461448 | tf_op jit(solution)/shard_map/ppermute | solution.py:313
  60.7 22.1 %collective-permute-done.3 = bf16[80,8,641]{2,1,0:T(8,128)(2,1)S(1)} collective-permute-done((bf16[80,8,641]{2,1,0:T(8,128)(2,1)S(1)}, bf16[80,8,641]{2,1,0:T(8,128)(2,1)S(1)}, u32[]{:S(2)}, u32[]{:S(2)}) %collective-permute-start.3) | collective-permute-done | bytes 820512 | tf_op jit(solution)/shard_map/ppermute | solution.py:313
  82.8 0.2 add_convert_fusion.1
  83.0 2.8 %collective-permute-start.4 = (bf16[40,8,641]{2,1,0:T(8,128)(2,1)S(1)}, bf16[40,8,641]{2,1,0:T(8,128)(2,1)S(1)}, u32[]{:S(2)}, u32[]{:S(2)}) collective-permute-start(bf16[40,8,641]{2,1,0:T(8,128)(2,1)S(1)} %add_convert_fusion.1), channel_id=1, source_target_pairs={{0,8},{2,10},{4,12},{6,14},{8,0},{10,2},{12,4},{14,6},{16,24},{18,... | collective-permute-start | bytes 1230728 | tf_op jit(solution)/shard_map/ppermute | solution.py:313
  85.8 10.7 %collective-permute-done.4 = bf16[40,8,641]{2,1,0:T(8,128)(2,1)S(1)} collective-permute-done((bf16[40,8,641]{2,1,0:T(8,128)(2,1)S(1)}, bf16[40,8,641]{2,1,0:T(8,128)(2,1)S(1)}, u32[]{:S(2)}, u32[]{:S(2)}) %collective-permute-start.4) | collective-permute-done | bytes 410272 | tf_op jit(solution)/shard_map/ppermute | solution.py:313
  96.4 0.1 add_convert_fusion.2
  96.6 2.8 %collective-permute-start.5 = (bf16[20,8,641]{2,1,0:T(8,128)(2,1)S(1)}, bf16[20,8,641]{2,1,0:T(8,128)(2,1)S(1)}, u32[]{:S(2)}, u32[]{:S(2)}) collective-permute-start(bf16[20,8,641]{2,1,0:T(8,128)(2,1)S(1)} %add_convert_fusion.2), channel_id=1, source_target_pairs={{0,16},{2,18},{4,20},{6,22},{8,24},{10,26},{12,28},{14,30},{16,0},... | collective-permute-start | bytes 615368 | tf_op jit(solution)/shard_map/ppermute | solution.py:313
  99.4 10.0 %collective-permute-done.5 = bf16[20,8,641]{2,1,0:T(8,128)(2,1)S(1)} collective-permute-done((bf16[20,8,641]{2,1,0:T(8,128)(2,1)S(1)}, bf16[20,8,641]{2,1,0:T(8,128)(2,1)S(1)}, u32[]{:S(2)}, u32[]{:S(2)}) %collective-permute-start.5) | collective-permute-done | bytes 205152 | tf_op jit(solution)/shard_map/ppermute | solution.py:313
  109.4 0.2 convert_add_fusion
  109.5 0.3 reshape.100
  109.8 0.4 fusion.15
  110.2 1.3 %collective-permute-start.6 = (f32[20,2,641]{2,1,0:T(2,128)S(1)}, f32[20,2,641]{2,1,0:T(2,128)S(1)}, u32[]{:S(2)}, u32[]{:S(2)}) collective-permute-start(f32[20,2,641]{2,1,0:T(2,128)S(1)} %get-tuple-element.10), channel_id=1, source_target_pairs={{1,0},{3,2},{5,4},{7,6},{9,8},{11,10},{13,12},{15,14},{17,16},{19,... | collective-permute-start | bytes 307688 | tf_op jit(solution)/shard_map/ppermute | solution.py:324
  111.5 0.3 stack_reshape.3
  111.8 5.2 %collective-permute-done.6 = f32[20,2,641]{2,1,0:T(2,128)S(1)} collective-permute-done((f32[20,2,641]{2,1,0:T(2,128)S(1)}, f32[20,2,641]{2,1,0:T(2,128)S(1)}, u32[]{:S(2)}, u32[]{:S(2)}) %collective-permute-start.6) | collective-permute-done | bytes 102592 | tf_op jit(solution)/shard_map/ppermute | solution.py:324
  117.0 0.2 fusion.2
  117.2 0.2 maximum_bitcast_fusion.1
  117.4 1.4 %maximum_bitcast_fusion = f32[4,2,2,20,641]{4,2,3,1,0:T(2,128)} fusion(f32[20,4,1,2,641]{4,3,0,2,1:T(2,128)S(1)} %maximum_bitcast_fusion.1, f32[20,4,1,2,641]{4,3,1,0,2:T(2,128)S(1)} %stack_reshape.3), kind=kLoop, calls=%fused_computation.1 | loop fusion | flops 205120 | bytes 1640960 | tf_op jit(solution)/shard_map/transpose | solution.py:334
  (11 shorter events, 0.0 us)
Async XLA Ops:
  0.6 5.9 %copy-start.3 = (s32[320]{0:T(512)S(1)}, s32[320]{0:T(512)}, u32[]{:S(2)}) copy-start(s32[320]{0:T(512)} %param.13) | copy-start | bytes 3844
  2.8 11.4 %collective-permute-start = (bf16[4,2,4096]{2,1,0:T(2,128)(2,1)}, bf16[4,2,4096]{2,1,0:T(2,128)(2,1)S(1)}, u32[]{:S(2)}, u32[]{:S(2)}) collective-permute-start(bf16[4,2,4096]{2,1,0:T(2,128)(2,1)} %get-tuple-element.6), channel_id=1, source_target_pairs={{0,2},{2,4},{4,6},{6,8},{8,10},{10,12},{12,14},{14,16},{16,18},{18... | collective-permute-start | bytes 196616 | tf_op jit(solution)/shard_map/ppermute | solution.py:291
  5.2 9.1 %collective-permute-start.1 = (bf16[4,2,4096]{2,1,0:T(2,128)(2,1)}, bf16[4,2,4096]{2,1,0:T(2,128)(2,1)S(1)}, u32[]{:S(2)}, u32[]{:S(2)}) collective-permute-start(bf16[4,2,4096]{2,1,0:T(2,128)(2,1)} %get-tuple-element.7), channel_id=1, source_target_pairs={{2,0},{4,2},{6,4},{8,6},{10,8},{12,10},{14,12},{16,14},{18,16},{20... | collective-permute-start | bytes 196616 | tf_op jit(solution)/shard_map/ppermute | solution.py:290
  14.2 0.6 copy-start.1
  14.2 0.6 copy-start.2
  49.7 8.7 %copy-start = (bf16[320,8,641]{2,1,0:T(8,128)(2,1)S(1)}, bf16[320,8,641]{2,1,0:T(8,128)(2,1)}, u32[]{:S(2)}) copy-start(bf16[320,8,641]{2,1,0:T(8,128)(2,1)} %legendre.1) | copy-start | bytes 9845764
  51.5 6.9 %collective-permute-start.2 = (bf16[160,8,641]{2,1,0:T(8,128)(2,1)S(1)}, bf16[160,8,641]{2,1,0:T(8,128)(2,1)S(1)}, u32[]{:S(2)}, u32[]{:S(2)}) collective-permute-start(bf16[160,8,641]{2,1,0:T(8,128)(2,1)S(1)} %slice.76), channel_id=1, source_target_pairs={{0,2},{2,0},{4,6},{6,4},{8,10},{10,8},{12,14},{14,12},{16,18},{18,... | collective-permute-start | bytes 4922888 | tf_op jit(solution)/shard_map/ppermute | solution.py:313
  58.6 24.1 %collective-permute-start.3 = (bf16[80,8,641]{2,1,0:T(8,128)(2,1)S(1)}, bf16[80,8,641]{2,1,0:T(8,128)(2,1)S(1)}, u32[]{:S(2)}, u32[]{:S(2)}) collective-permute-start(bf16[80,8,641]{2,1,0:T(8,128)(2,1)S(1)} %add_convert_fusion), channel_id=1, source_target_pairs={{0,4},{2,6},{4,0},{6,2},{8,12},{10,14},{12,8},{14,10},{16,20},{18,... | collective-permute-start | bytes 2461448 | tf_op jit(solution)/shard_map/ppermute | solution.py:313
  83.0 26.9 %copy-start.4 = (f32[4]{0:T(128)S(1)}, f32[4]{0:T(128)}, u32[]{:S(2)}) copy-start(f32[4]{0:T(128)} %param.11) | copy-start | bytes 52
  83.0 13.5 %collective-permute-start.4 = (bf16[40,8,641]{2,1,0:T(8,128)(2,1)S(1)}, bf16[40,8,641]{2,1,0:T(8,128)(2,1)S(1)}, u32[]{:S(2)}, u32[]{:S(2)}) collective-permute-start(bf16[40,8,641]{2,1,0:T(8,128)(2,1)S(1)} %add_convert_fusion.1), channel_id=1, source_target_pairs={{0,8},{2,10},{4,12},{6,14},{8,0},{10,2},{12,4},{14,6},{16,24},{18,... | collective-permute-start | bytes 1230728 | tf_op jit(solution)/shard_map/ppermute | solution.py:313
  96.6 12.8 %collective-permute-start.5 = (bf16[20,8,641]{2,1,0:T(8,128)(2,1)S(1)}, bf16[20,8,641]{2,1,0:T(8,128)(2,1)S(1)}, u32[]{:S(2)}, u32[]{:S(2)}) collective-permute-start(bf16[20,8,641]{2,1,0:T(8,128)(2,1)S(1)} %add_convert_fusion.2), channel_id=1, source_target_pairs={{0,16},{2,18},{4,20},{6,22},{8,24},{10,26},{12,28},{14,30},{16,0},... | collective-permute-start | bytes 615368 | tf_op jit(solution)/shard_map/ppermute | solution.py:313
  110.2 6.8 %collective-permute-start.6 = (f32[20,2,641]{2,1,0:T(2,128)S(1)}, f32[20,2,641]{2,1,0:T(2,128)S(1)}, u32[]{:S(2)}, u32[]{:S(2)}) collective-permute-start(f32[20,2,641]{2,1,0:T(2,128)S(1)} %get-tuple-element.10), channel_id=1, source_target_pairs={{1,0},{3,2},{5,4},{7,6},{9,8},{11,10},{13,12},{15,14},{17,16},{19,... | collective-permute-start | bytes 307688 | tf_op jit(solution)/shard_map/ppermute | solution.py:324

commit v2 on v1

--- a/solution.py
+++ b/solution.py
@@ -11,6 +11,7 @@
 
 GROUP = 8
 LANES = 128
+WIDTH = 256
 
 
 def edge_kernel(first_ref, last_ref, head_ref, tail_ref):
@@ -30,6 +31,7 @@
         ],
         out_specs=[pl.BlockSpec((levels, 2, lon), lambda i: (0, 0, 0))] * 2,
         out_shape=[jax.ShapeDtypeStruct((levels, 2, lon), air.dtype)] * 2,
+        compiler_params=pltpu.CompilerParams(vmem_limit_bytes=8 << 20),
         name="edges",
     )(air, air)
 
@@ -70,6 +72,7 @@
         in_specs=[spec] * 4,
         out_specs=pl.BlockSpec((1, 2, count // 2, half), lambda i, j: (i, 0, j, 0)),
         out_shape=jax.ShapeDtypeStruct((4, 2, count, half), jnp.bfloat16),
+        compiler_params=pltpu.CompilerParams(vmem_limit_bytes=8 << 20),
         cost_estimate=pl.CostEstimate(
             flops=4 * 2 * count * half * 3, bytes_accessed=4 * 2 * count * half * 2, transcendentals=0
         ),
@@ -136,6 +139,7 @@
             jax.ShapeDtypeStruct((2, 2, levels, rows, lon // 2), jnp.bfloat16),
         ],
         scratch_shapes=[pltpu.VMEM((2, rows + 16, lon), jnp.float32)],
+        compiler_params=pltpu.CompilerParams(vmem_limit_bytes=12 << 20),
         cost_estimate=pl.CostEstimate(
             flops=20 * air.size, bytes_accessed=7 * air.size, transcendentals=0
         ),
@@ -199,7 +203,7 @@
         out_specs=pl.BlockSpec((pairs // GROUP, 1, blocks * 2 * GROUP, wide), lambda i: (0, i, 0, 0)),
         out_shape=jax.ShapeDtypeStruct((pairs // GROUP, 2, blocks * 2 * GROUP, wide), jnp.bfloat16),
         scratch_shapes=[pltpu.VMEM((pl.cdiv(width, LANES), 2, pairs, LANES), jnp.float32)],
-        compiler_params=pltpu.CompilerParams(vmem_limit_bytes=60 << 20),
+        compiler_params=pltpu.CompilerParams(vmem_limit_bytes=24 << 20),
         cost_estimate=pl.CostEstimate(
             flops=2 * 8 * count * half * width,
             bytes_accessed=2 * (waves.size + folds.size),
@@ -209,61 +213,87 @@
     )(waves, folds)
 
 
-def legendre_kernel(place_ref, block_ref, table_ref, out_ref, turned):
+def legendre_kernel(
+    half_k, start, extra, place_ref, block_ref, table_ref, keep_ref, send_ref, spectra, turned, sems
+):
     step = pl.program_id(0)
-    rows, pairs, columns = table_ref.shape
+    rows, pairs, width = table_ref.shape
     groups = pairs // GROUP
-    channels = out_ref.shape[1]
+    _, channels, kept = spectra.shape
+    slots = place_ref[half_k]
+    lane = lax.broadcasted_iota(jnp.int32, (channels, LANES), 1)
     for group in range(groups):
-        table = table_ref[:, group * GROUP : (group + 1) * GROUP, :].reshape(rows * GROUP, columns)
+        table = table_ref[:, group * GROUP : (group + 1) * GROUP, :].reshape(rows * GROUP, width)
         left = block_ref[group].reshape(4 * channels * GROUP, rows * GROUP)
         sums = jnp.dot(left, table, preferred_element_type=jnp.float32)
-        sums = sums.reshape(2, 2, channels, GROUP, columns)
+        sums = sums.reshape(2, 2, channels, GROUP, width)
         first_pair = (step * groups + group) * GROUP
-        pair = first_pair + lax.broadcasted_iota(jnp.int32, (GROUP, columns), 0)
-        column = lax.broadcasted_iota(jnp.int32, (GROUP, columns), 1)
-        first = column < columns - 1 - pair
-        odd = jnp.where(first, column, column - (columns - 1) + pair) & 1
+        pair = first_pair + lax.broadcasted_iota(jnp.int32, (GROUP, width), 0)
+        column = start + lax.broadcasted_iota(jnp.int32, (GROUP, width), 1)
+        first = column < 2 * half_k - pair
+        odd = jnp.where(first, column, column - 2 * half_k + pair) & 1
         even = (odd == 0)[None]
         chosen = jnp.where(
             first[None],
             jnp.where(even, sums[0, 0], sums[0, 1]),
             jnp.where(even, sums[1, 0], sums[1, 1]),
         )
-        chosen = chosen.reshape(channels * GROUP, columns)
-        for tile in range(turned.shape[0]):
-            start, end = tile * LANES, min(columns, (tile + 1) * LANES)
-            turned[tile, :, : end - start] = chosen[:, start:end]
+        chosen = chosen.reshape(channels * GROUP, width)
+        for tile in range(width // LANES):
+            turned[group, tile] = chosen[:, tile * LANES : (tile + 1) * LANES]
         for member in range(GROUP):
             place = place_ref[first_pair + member]
-            for tile in range(turned.shape[0]):
-                start, end = tile * LANES, min(columns, (tile + 1) * LANES)
-                value = turned[tile, pl.ds(member, channels, stride=GROUP), :]
-                out_ref[place, :, start:end] = value[:, : end - start].astype(out_ref.dtype)
-
-
-def legendre(places, blocks, table):
-    rows, half_k, columns = table.shape
+            for tile in range(kept // LANES):
+                value = turned[group, tile, pl.ds(member, channels, stride=GROUP), :]
+                spectra[place, :, tile * LANES : (tile + 1) * LANES] = value.astype(spectra.dtype)
+            if extra:
+                chunk = place // (slots + 1)
+                within = place - chunk * (slots + 1)
+                spare = chunk * (slots + 1) + slots
+                value = turned[group, kept // LANES, pl.ds(member, channels, stride=GROUP), :]
+                value = jnp.broadcast_to(value[:, :1], (channels, LANES)).astype(spectra.dtype)
+                before = spectra[spare, :, :LANES]
+                spectra[spare, :, :LANES] = jnp.where(lane == within, value, before)
+
+    @pl.when(step == pl.num_programs(0) - 1)
+    def _():
+        count = spectra.shape[0] // 2
+        send = pltpu.make_async_copy(spectra.at[pl.ds(count, count)], send_ref, sems.at[0])
+        keep = pltpu.make_async_copy(spectra.at[pl.ds(0, count)], keep_ref, sems.at[1])
+        send.start()
+        keep.start()
+        send.wait()
+        keep.wait()
+
+
+def legendre(places, blocks, table, start, kept, extra, total):
+    rows, half_k, _ = table.shape
     channels = blocks.shape[1] * blocks.shape[2] // (4 * GROUP)
-    pairs = 2 * GROUP
+    pairs = 8 * GROUP
     groups = pairs // GROUP
-    return pl.pallas_call(
-        legendre_kernel,
+    width = kept + (LANES if extra else 0)
+    result = jax.ShapeDtypeStruct((total // 2, channels, kept), jnp.bfloat16)
+    return pl.pallas_call(
+        functools.partial(legendre_kernel, half_k, start, extra),
         grid_spec=pltpu.PrefetchScalarGridSpec(
             num_scalar_prefetch=1,
             grid=(half_k // pairs,),
             in_specs=[
                 pl.BlockSpec((groups, *blocks.shape[1:]), lambda i, s: (i, 0, 0, 0)),
-                pl.BlockSpec((rows, pairs, columns), lambda i, s: (0, i, 0)),
+                pl.BlockSpec((rows, pairs, width), lambda i, s: (0, i, start // width)),
             ],
-            out_specs=pl.BlockSpec((half_k, channels, columns), lambda i, s: (0, 0, 0)),
-            scratch_shapes=[pltpu.VMEM((pl.cdiv(columns, LANES), channels * GROUP, LANES), jnp.float32)],
-        ),
-        out_shape=jax.ShapeDtypeStruct((half_k, channels, columns), jnp.bfloat16),
-        compiler_params=pltpu.CompilerParams(vmem_limit_bytes=60 << 20),
+            out_specs=[pl.BlockSpec(memory_space=pl.ANY)] * 2,
+            scratch_shapes=[
+                pltpu.VMEM((total, channels, kept), jnp.bfloat16),
+                pltpu.VMEM((groups, width // LANES, channels * GROUP, LANES), jnp.float32),
+                pltpu.SemaphoreType.DMA((2,)),
+            ],
+        ),
+        out_shape=[result, result],
+        compiler_params=pltpu.CompilerParams(vmem_limit_bytes=24 << 20),
         cost_estimate=pl.CostEstimate(
-            flops=2 * blocks.size * columns,
-            bytes_accessed=2 * (blocks.size + table.size),
+            flops=2 * blocks.size * width,
+            bytes_accessed=2 * (blocks.size + rows * half_k * width),
             transcendentals=0,
         ),
         name="legendre",
@@ -297,24 +327,39 @@
     down = jnp.sin(row * (math.pi / steps)) / centre
     is_last = (band == bands - 1).astype(jnp.int32)[None]
     slot = jnp.arange(half_k, dtype=jnp.int32)
-    place = reversed_bits((slot // slots) ^ band, bits) * slots + slot % slots
-    places = jnp.sum(
-        jnp.where(mode_degree[None, :] == slot[:, None], place[None, :], 0), axis=1, dtype=jnp.int32
-    )
+    here = mode_degree[None, :] == slot[:, None]
+    chunk = reversed_bits((slot // slots) ^ band, bits)
+
+    def places_with(stride):
+        place = chunk * stride + slot % slots
+        found = jnp.sum(jnp.where(here, place[None, :], 0), axis=1, dtype=jnp.int32)
+        return jnp.concatenate([found, jnp.full((1,), slots, jnp.int32)])
 
     smoothed, folds = smooth(air, kappa, above, below, up, down, is_last)
     blocks = fourier_blocks(waves, folds.reshape(2, 2 * levels * rows, lon // 2), rows)
-    held = [legendre(places, blocks, table)]
-    count = half_k
-    for bit in range(bits):
-        count //= 2
-        outgoing = sum(part[count : 2 * count].astype(jnp.float32) for part in held)
-        held.append(
-            lax.ppermute(
-                outgoing.astype(jnp.bfloat16), "band", [(i, i ^ (1 << bit)) for i in range(bands)]
+    pieces = []
+    top = columns - 1
+    for start in range(0, top, WIDTH):
+        kept = min(WIDTH, top - start)
+        extra = start + kept == top
+        stride = slots + 1 if extra else slots
+        keep, count = legendre(
+            places_with(stride), blocks, table, start, kept, extra, stride * bands
+        ), stride * bands // 2
+        held, outgoing = [keep[0]], keep[1]
+        for bit in range(bits):
+            held.append(
+                lax.ppermute(outgoing, "band", [(i, i ^ (1 << bit)) for i in range(bands)])
             )
-        )
-    mine = sum(part[:slots].astype(jnp.float32) for part in held)
+            count //= 2
+            if bit < bits - 1:
+                outgoing = sum(part[count : 2 * count].astype(jnp.float32) for part in held)
+                outgoing = outgoing.astype(jnp.bfloat16)
+        done = sum(part[:stride].astype(jnp.float32) for part in held)
+        pieces.append(done[:slots])
+        if extra:
+            pieces.append(jnp.swapaxes(done[slots, :, :slots], 0, 1)[:, :, None])
+    mine = jnp.concatenate(pieces, axis=2)
     mine = mine.reshape(slots, levels, 2, columns)
     weighted = depth[None, :, None, None] * mine
     levs = lax.axis_size("lev")

time: 120 us -> 91.6 us (0.76)
  waiting for transfers between devices: 51.5 us -> 28.9 us
  Pallas kernels: 43.1 us -> 25.4 us
  starting transfers between devices: 15.9 us -> 21.1 us
  local copies, waits for them, and re-layouts: 3.04 us -> 6.76 us
  other arithmetic: 4.5 us -> 8.11 us
    ppermute x4 -> x12, waiting for transfers between devices: 46.3 us -> 23.7 us  [on_device(): lax.ppermute(outgoing, 'band', [(i, i ^ 1 << bit) for i in range(bands)])]
    pallas_call x1 -> x3, Pallas kernels: 20 us -> 13.4 us  [legendre(): pl.pallas_call(functools.partial(legendre_kernel, half_k, start, extra),...]
    ppermute x4 -> x12, starting transfers between devices: 10.9 us -> 16 us  [on_device(): lax.ppermute(outgoing, 'band', [(i, i ^ 1 << bit) for i in range(bands)])]
    unnamed x10 -> x20, local copies, waits for them, and re-layouts: 0.65 us -> 5.49 us
    pallas_call x1, Pallas kernels: 6.23 us -> 1.87 us  [wave_table(): pl.pallas_call(wave_kernel, grid=(4, 2), in_specs=[spec] * 4, out_specs=p...]
    pallas_call x1, Pallas kernels: 7.42 us -> 3.84 us  [fourier_blocks(): pl.pallas_call(functools.partial(fourier_kernel, rows), grid=(2,), in_spe...]
    convert_element_type x3 -> x9, other arithmetic: 0.61 us -> 2.59 us  [on_device(): outgoing = outgoing.astype(jnp.bfloat16)]
    slice x1 -> x2, local copies, waits for them, and re-layouts: 1.82 us -> 0.01 us  [the longest x1 0.01 us: on_device(): pieces.append(done[:slots])]
  transfers between devices with their start and end apart: 7 -> 15, of which waited for: 5 -> 8; matrix products, arithmetic and copies ran while one was open for 1% -> 6% of each run, Pallas kernels for 5% -> 11%
where the time goes in v2:
time: 91.6 us; the launch traced here: 91.2 us
  waiting for transfers between devices  28.9 us (32%)
  Pallas kernels  25.4 us (28%)
  starting transfers between devices  21.1 us (23%)
  other arithmetic  8.11 us (9%)
  local copies, waits for them, and re-layouts  6.76 us (7%)
    ppermute x12, waiting for transfers between devices, on_device(): lax.ppermute(outgoing, 'band', [(i, i ^ 1 << bit) for i in range(bands)])  23.7 us
    ppermute x12, starting transfers between devices, on_device(): lax.ppermute(outgoing, 'band', [(i, i ^ 1 << bit) for i in range(bands)])  16 us
    pallas_call x3, Pallas kernels, legendre(): pl.pallas_call(functools.partial(legendre_kernel, half_k, start, extra),...  13.4 us
    pallas_call x1, Pallas kernels, smooth(): pl.pallas_call(smooth_kernel, grid=(levels,), in_specs=[pl.BlockSpec(memo...  5.84 us
    unnamed x20, local copies, waits for them, and re-layouts  5.49 us
    ppermute x1, waiting for transfers between devices, on_device(): lower = lax.ppermute(total, 'lev', [(i + 1, i) for i in range(levs - 1)])  5.14 us
    pallas_call x1, Pallas kernels, fourier_blocks(): pl.pallas_call(functools.partial(fourier_kernel, rows), grid=(2,), in_spe...  3.84 us
    convert_element_type x9, other arithmetic, on_device(): outgoing = outgoing.astype(jnp.bfloat16)  2.59 us
  transfers between devices with their start and end apart: 15, of which 8 were waited for; matrix products, arithmetic and copies ran while one was open for 6% of the time, Pallas kernels for 11%

profile of v2, /device:TPU:0, one launch (start us, length us, event | category | flops | bytes accessed | tf_op | source)
XLA Modules:
  0.0 91.2 jit_solution(17725271561424452214)
XLA Ops:
  0.6 1.6 %copy-done.1 = bf16[4,2,32,4096]{3,2,1,0:T(8,128)(2,1)S(1)} copy-done((bf16[4,2,32,4096]{3,2,1,0:T(8,128)(2,1)S(1)}, bf16[4,2,32,4096]{3,2,1,0:T(8,128)(2,1)}, u32[]{:S(2)}) %copy-start.1) | copy-done | bytes 2097176
  2.7 2.5 %collective-permute-start = (bf16[4,2,4096]{2,1,0:T(2,128)(2,1)S(1)}, bf16[4,2,4096]{2,1,0:T(2,128)(2,1)S(1)}, u32[]{:S(2)}, u32[]{:S(2)}) collective-permute-start(bf16[4,2,4096]{2,1,0:T(2,128)(2,1)S(1)} %get-tuple-element.12), channel_id=1, source_target_pairs={{0,2},{2,4},{4,6},{6,8},{8,10},{10,12},{12,14},{14,16},{16,18},{18... | collective-permute-start | bytes 196616 | tf_op jit(solution)/shard_map/ppermute | solution.py:321
  5.2 1.3 %collective-permute-start.1 = (bf16[4,2,4096]{2,1,0:T(2,128)(2,1)S(1)}, bf16[4,2,4096]{2,1,0:T(2,128)(2,1)S(1)}, u32[]{:S(2)}, u32[]{:S(2)}) collective-permute-start(bf16[4,2,4096]{2,1,0:T(2,128)(2,1)S(1)} %get-tuple-element.13), channel_id=1, source_target_pairs={{2,0},{4,2},{6,4},{8,6},{10,8},{12,10},{14,12},{16,14},{18,16},{20... | collective-permute-start | bytes 196616 | tf_op jit(solution)/shard_map/ppermute | solution.py:320
  7.7 1.0 %copy-done.4 = f32[4,160,128]{2,1,0:T(8,128)S(1)} copy-done((f32[4,160,128]{2,1,0:T(8,128)S(1)}, f32[4,160,128]{2,1,0:T(8,128)}, u32[]{:S(2)}) %copy-start.4) | copy-done | bytes 327704
  8.7 1.0 %copy-done.5 = f32[4,160,128]{2,1,0:T(8,128)S(1)} copy-done((f32[4,160,128]{2,1,0:T(8,128)S(1)}, f32[4,160,128]{2,1,0:T(8,128)}, u32[]{:S(2)}) %copy-start.5) | copy-done | bytes 327704
  9.6 1.0 %copy-done.6 = f32[4,160,128]{2,1,0:T(8,128)S(1)} copy-done((f32[4,160,128]{2,1,0:T(8,128)S(1)}, f32[4,160,128]{2,1,0:T(8,128)}, u32[]{:S(2)}) %copy-start.6) | copy-done | bytes 327704
  10.6 1.0 %copy-done.7 = f32[4,160,128]{2,1,0:T(8,128)S(1)} copy-done((f32[4,160,128]{2,1,0:T(8,128)S(1)}, f32[4,160,128]{2,1,0:T(8,128)}, u32[]{:S(2)}) %copy-start.7) | copy-done | bytes 327704
  11.6 1.9 %waves.1.wave_ref = bf16[4,2,160,2048]{3,2,1,0:T(8,128)(2,1)S(1)} custom-call(f32[4,160,128]{2,1,0:T(8,128)S(1)} %copy-done.4, f32[4,160,128]{2,1,0:T(8,128)S(1)} %copy-done.5, f32[4,160,128]{2,1,0:T(8,128)S(1)} %copy-done.6, f32[4,160,128]{2,1,0:T(8,128)S(1)} %copy-done.7), custom_call_target="tpu_custom_call" | custom-call | flops 7864320 | bytes 5242880 | tf_op jit(solution)/shard_map/waves/pallas_call | solution.py:69
  13.6 5.8 %smooth.1 = (bf16[4,2,32,4096]{3,2,1,0:T(8,128)(2,1)}, bf16[2,2,4,32,2048]{4,3,2,1,0:T(8,128)(2,1)S(1)}) custom-call(s32[1]{0:T(128)} %bitcast.last_ref, bf16[4,2,32,4096]{3,2,1,0:T(8,128)(2,1)S(1)} %copy-done.2, bf16[2,32,4096]{2,1,0:T(8,128)(2,1)S(1)} %copy-done.3, bf16[4,2,4096]{2,1,0:T(2,128)(2,1)S(1)} %collective-permute-done.above_ref, ...), custom_call_target="tpu_custom_call" | custom-call | flops 20971520 | bytes 7340032 | tf_op jit(solution)/shard_map/smooth/pallas_call | solution.py:121
  19.4 3.8 %fourier.1.block_ref = bf16[40,2,128,256]{3,2,1,0:T(8,128)(2,1)S(1)} custom-call(bf16[4,2,160,2048]{3,2,1,0:T(8,128)(2,1)S(1)} %waves.1.wave_ref, bf16[2,256,2048]{2,1,0:T(8,128)(2,1)S(1)} %bitcast.57), custom_call_target="tpu_custom_call" | custom-call | flops 1342177280 | bytes 7340032 | tf_op jit(solution)/shard_map/fourier/pallas_call | solution.py:196
  23.3 5.6 %legendre.5 = (bf16[168,8,128]{2,1,0:T(8,128)(2,1)S(1)}, bf16[168,8,128]{2,1,0:T(8,128)(2,1)S(1)}) custom-call(s32[321]{0:T(512)S(1)} %pad_add_fusion.place_ref, bf16[40,2,128,256]{3,2,1,0:T(8,128)(2,1)S(1)} %fourier.1.block_ref, bf16[32,320,641]{2,1,0:T(8,128)(2,1)S(1)} %copy-done), custom_call_target="tpu_custom_call" | custom-call | flops 1342177280 | bytes 10485760 | tf_op jit(solution)/shard_map/legendre/pallas_call | solution.py:276
  28.9 3.3 %collective-permute-start.10 = (bf16[168,8,128]{2,1,0:T(8,128)(2,1)S(1)}, bf16[168,8,128]{2,1,0:T(8,128)(2,1)S(1)}, u32[]{:S(2)}, u32[]{:S(2)}) collective-permute-start(bf16[168,8,128]{2,1,0:T(8,128)(2,1)S(1)} %get-tuple-element.21), channel_id=1, source_target_pairs={{0,2},{2,0},{4,6},{6,4},{8,10},{10,8},{12,14},{14,12},{16,18},{18,... | collective-permute-start | bytes 1032200 | tf_op jit(solution)/shard_map/ppermute | solution.py:352
  32.2 1.2 %collective-permute-done.10 = bf16[168,8,128]{2,1,0:T(8,128)(2,1)S(1)} collective-permute-done((bf16[168,8,128]{2,1,0:T(8,128)(2,1)S(1)}, bf16[168,8,128]{2,1,0:T(8,128)(2,1)S(1)}, u32[]{:S(2)}, u32[]{:S(2)}) %collective-permute-start.10) | collective-permute-done | bytes 344096 | tf_op jit(solution)/shard_map/ppermute | solution.py:352
  33.5 2.1 %collective-permute-start.11 = (bf16[84,8,128]{2,1,0:T(8,128)(2,1)S(1)}, bf16[84,8,128]{2,1,0:T(8,128)(2,1)S(1)}, u32[]{:S(2)}, u32[]{:S(2)}) collective-permute-start(bf16[84,8,128]{2,1,0:T(8,128)(2,1)S(1)} %add_convert_fusion.2), channel_id=1, source_target_pairs={{0,4},{2,6},{4,0},{6,2},{8,12},{10,14},{12,8},{14,10},{16,20},{18,... | collective-permute-start | bytes 516104 | tf_op jit(solution)/shard_map/ppermute | solution.py:352
  35.5 3.9 %legendre.4 = (bf16[160,8,256]{2,1,0:T(8,128)(2,1)S(1)}, bf16[160,8,256]{2,1,0:T(8,128)(2,1)S(1)}) custom-call(s32[321]{0:T(512)S(1)} %pad_add_fusion.1.place_ref, bf16[40,2,128,256]{3,2,1,0:T(8,128)(2,1)S(1)} %fourier.1.block_ref, bf16[32,320,641]{2,1,0:T(8,128)(2,1)S(1)} %copy-done), custom_call_target="tpu_custom_call" | custom-call | flops 1342177280 | bytes 10485760 | tf_op jit(solution)/shard_map/legendre/pallas_call | solution.py:276
  39.5 3.9 %legendre.3 = (bf16[160,8,256]{2,1,0:T(8,128)(2,1)S(1)}, bf16[160,8,256]{2,1,0:T(8,128)(2,1)S(1)}) custom-call(s32[321]{0:T(512)S(1)} %pad_add_fusion.1.place_ref, bf16[40,2,128,256]{3,2,1,0:T(8,128)(2,1)S(1)} %fourier.1.block_ref, bf16[32,320,641]{2,1,0:T(8,128)(2,1)S(1)} %copy-done), custom_call_target="tpu_custom_call" | custom-call | flops 1342177280 | bytes 10485760 | tf_op jit(solution)/shard_map/legendre/pallas_call | solution.py:276
  44.1 1.6 %collective-permute-start.12 = (bf16[42,8,128]{2,1,0:T(8,128)(2,1)S(1)}, bf16[42,8,128]{2,1,0:T(8,128)(2,1)S(1)}, u32[]{:S(2)}, u32[]{:S(2)}) collective-permute-start(bf16[42,8,128]{2,1,0:T(8,128)(2,1)S(1)} %add_convert_fusion.5), channel_id=1, source_target_pairs={{0,8},{2,10},{4,12},{6,14},{8,0},{10,2},{12,4},{14,6},{16,24},{18,... | collective-permute-start | bytes 258056 | tf_op jit(solution)/shard_map/ppermute | solution.py:352
  45.7 2.9 %collective-permute-done.12 = bf16[42,8,128]{2,1,0:T(8,128)(2,1)S(1)} collective-permute-done((bf16[42,8,128]{2,1,0:T(8,128)(2,1)S(1)}, bf16[42,8,128]{2,1,0:T(8,128)(2,1)S(1)}, u32[]{:S(2)}, u32[]{:S(2)}) %collective-permute-start.12) | collective-permute-done | bytes 86048 | tf_op jit(solution)/shard_map/ppermute | solution.py:352
  48.6 2.7 %collective-permute-start.13 = (bf16[21,8,128]{2,1,0:T(8,128)(2,1)S(1)}, bf16[21,8,128]{2,1,0:T(8,128)(2,1)S(1)}, u32[]{:S(2)}, u32[]{:S(2)}) collective-permute-start(bf16[21,8,128]{2,1,0:T(8,128)(2,1)S(1)} %add_convert_fusion.8), channel_id=1, source_target_pairs={{0,16},{2,18},{4,20},{6,22},{8,24},{10,26},{12,28},{14,30},{16,0},... | collective-permute-start | bytes 129032 | tf_op jit(solution)/shard_map/ppermute | solution.py:352
  52.1 1.4 %collective-permute-start.7 = (bf16[80,8,256]{2,1,0:T(8,128)(2,1)}, bf16[80,8,256]{2,1,0:T(8,128)(2,1)S(1)}, u32[]{:S(2)}, u32[]{:S(2)}) collective-permute-start(bf16[80,8,256]{2,1,0:T(8,128)(2,1)} %add_convert_fusion), channel_id=1, source_target_pairs={{0,4},{2,6},{4,0},{6,2},{8,12},{10,14},{12,8},{14,10},{16,20},{18,... | collective-permute-start | bytes 983048 | tf_op jit(solution)/shard_map/ppermute | solution.py:352
  55.8 7.1 %collective-permute-done.7 = bf16[80,8,256]{2,1,0:T(8,128)(2,1)S(1)} collective-permute-done((bf16[80,8,256]{2,1,0:T(8,128)(2,1)}, bf16[80,8,256]{2,1,0:T(8,128)(2,1)S(1)}, u32[]{:S(2)}, u32[]{:S(2)}) %collective-permute-start.7) | collective-permute-done | bytes 327712 | tf_op jit(solution)/shard_map/ppermute | solution.py:352
  63.0 1.6 %collective-permute-start.8 = (bf16[40,8,256]{2,1,0:T(8,128)(2,1)S(1)}, bf16[40,8,256]{2,1,0:T(8,128)(2,1)S(1)}, u32[]{:S(2)}, u32[]{:S(2)}) collective-permute-start(bf16[40,8,256]{2,1,0:T(8,128)(2,1)S(1)} %add_convert_fusion.3), channel_id=1, source_target_pairs={{0,8},{2,10},{4,12},{6,14},{8,0},{10,2},{12,4},{14,6},{16,24},{18,... | collective-permute-start | bytes 491528 | tf_op jit(solution)/shard_map/ppermute | solution.py:352
  64.6 2.9 %collective-permute-done.3 = bf16[80,8,256]{2,1,0:T(8,128)(2,1)S(1)} collective-permute-done((bf16[80,8,256]{2,1,0:T(8,128)(2,1)}, bf16[80,8,256]{2,1,0:T(8,128)(2,1)S(1)}, u32[]{:S(2)}, u32[]{:S(2)}) %collective-permute-start.3) | collective-permute-done | bytes 327712 | tf_op jit(solution)/shard_map/ppermute | solution.py:352
  67.6 1.6 %collective-permute-start.4 = (bf16[40,8,256]{2,1,0:T(8,128)(2,1)S(1)}, bf16[40,8,256]{2,1,0:T(8,128)(2,1)S(1)}, u32[]{:S(2)}, u32[]{:S(2)}) collective-permute-start(bf16[40,8,256]{2,1,0:T(8,128)(2,1)S(1)} %add_convert_fusion.4), channel_id=1, source_target_pairs={{0,8},{2,10},{4,12},{6,14},{8,0},{10,2},{12,4},{14,6},{16,24},{18,... | collective-permute-start | bytes 491528 | tf_op jit(solution)/shard_map/ppermute | solution.py:352
  69.7 4.0 %collective-permute-done.4 = bf16[40,8,256]{2,1,0:T(8,128)(2,1)S(1)} collective-permute-done((bf16[40,8,256]{2,1,0:T(8,128)(2,1)S(1)}, bf16[40,8,256]{2,1,0:T(8,128)(2,1)S(1)}, u32[]{:S(2)}, u32[]{:S(2)}) %collective-permute-start.4) | collective-permute-done | bytes 163872 | tf_op jit(solution)/shard_map/ppermute | solution.py:352
  74.4 2.5 %collective-permute-done.9 = bf16[20,8,256]{2,1,0:T(8,128)(2,1)S(1)} collective-permute-done((bf16[20,8,256]{2,1,0:T(8,128)(2,1)S(1)}, bf16[20,8,256]{2,1,0:T(8,128)(2,1)S(1)}, u32[]{:S(2)}, u32[]{:S(2)}) %collective-permute-start.9) | collective-permute-done | bytes 81952 | tf_op jit(solution)/shard_map/ppermute | solution.py:352
  77.1 3.0 %collective-permute-done.5 = bf16[20,8,256]{2,1,0:T(8,128)(2,1)} collective-permute-done((bf16[20,8,256]{2,1,0:T(8,128)(2,1)}, bf16[20,8,256]{2,1,0:T(8,128)(2,1)}, u32[]{:S(2)}, u32[]{:S(2)}) %collective-permute-start.5) | collective-permute-done | bytes 81952 | tf_op jit(solution)/shard_map/ppermute | solution.py:352
  80.1 1.0 %convert_add_fusion.1 = f32[20,8,256]{2,1,0:T(8,128)S(1)} fusion(bf16[20,8,256]{2,1,0:T(8,128)(2,1)} %collective-permute-done.5, bf16[40,8,256]{2,1,0:T(8,128)(2,1)} %copy-done.8, bf16[80,8,256]{2,1,0:T(8,128)(2,1)S(1)} %collective-permute-done.3, bf16[160,8,256]{2,1,0:T(8,128)(2,1)S(1)} %collective-permute-done.2, bf16[160,8,256]{2,1,0:T(8,128)(2,1)S(1)} %get-tuple-element.16), kind=kLoop, calls=%fused_computation.14 | loop fusion | flops 368640 | bytes 573440 | tf_op jit(solution)/shard_map/add | solution.py:358
  81.2 1.3 %fusion.14 = (f32[20,2,641]{2,1,0:T(2,128)S(1)}, f32[20,4,2,641]{3,2,0,1:T(2,128)S(1)}) fusion(f32[20,4,2,1]{3,2,0,1:T(2,128)} %copy.35, f32[4]{0:T(128)S(1)} %copy-done.9, f32[20,4,2,256]{3,2,1,0:T(2,128)S(1)} %concatenate.37, f32[20,4,2,256]{3,2,1,0:T(2,128)S(1)} %concatenate.38, f32[20,4,2,128]{3,2,1,0:T(2,128)S(1)} %bitcast.58), kind=kLoop, calls=%fused_computation.51 | loop fusion | flops 487160 | bytes 923056 | tf_op jit(solution)/shard_map/reduce_sum | solution.py:366
  82.5 1.3 %collective-permute-start.14 = (f32[20,2,641]{2,1,0:T(2,128)S(1)}, f32[20,2,641]{2,1,0:T(2,128)S(1)}, u32[]{:S(2)}, u32[]{:S(2)}) collective-permute-start(f32[20,2,641]{2,1,0:T(2,128)S(1)} %get-tuple-element.24), channel_id=1, source_target_pairs={{1,0},{3,2},{5,4},{7,6},{9,8},{11,10},{13,12},{15,14},{17,16},{19,... | collective-permute-start | bytes 307688 | tf_op jit(solution)/shard_map/ppermute | solution.py:369
  84.1 5.1 %collective-permute-done.14 = f32[20,2,641]{2,1,0:T(2,128)S(1)} collective-permute-done((f32[20,2,641]{2,1,0:T(2,128)S(1)}, f32[20,2,641]{2,1,0:T(2,128)S(1)}, u32[]{:S(2)}, u32[]{:S(2)}) %collective-permute-start.14) | collective-permute-done | bytes 102592 | tf_op jit(solution)/shard_map/ppermute | solution.py:369
  89.8 1.4 %maximum_bitcast_fusion = f32[4,2,2,20,641]{4,2,3,1,0:T(2,128)} fusion(f32[20,4,1,2,641]{4,3,0,2,1:T(2,128)S(1)} %maximum_bitcast_fusion.1, f32[20,4,1,2,1]{4,3,0,2,1:T(2,128)S(1)} %copy.31, f32[20,4,1,2,256]{4,3,1,0,2:T(2,128)S(1)} %concatenate.31, f32[20,4,1,2,256]{4,3,1,0,2:T(2,128)S(1)} %concatenate.32, f32[20,4,1,2,128]{4,3,1,0,2:T(2,128)S(1)} %bitcast.59), kind=kLoop, calls=%fused_computation | loop fusion | flops 820480 | bytes 1640960 | tf_op jit(solution)/shard_map/transpose | solution.py:379
  (54 shorter events, 7.8 us)
Async XLA Ops:
  0.6 1.6 %copy-start.1 = (bf16[4,2,32,4096]{3,2,1,0:T(8,128)(2,1)S(1)}, bf16[4,2,32,4096]{3,2,1,0:T(8,128)(2,1)}, u32[]{:S(2)}) copy-start(bf16[4,2,32,4096]{3,2,1,0:T(8,128)(2,1)} %air_ref.1) | copy-start | bytes 6291460
  2.2 11.3 %copy-start.2 = (bf16[4,2,32,4096]{3,2,1,0:T(8,128)(2,1)S(1)}, bf16[4,2,32,4096]{3,2,1,0:T(8,128)(2,1)}, u32[]{:S(2)}) copy-start(bf16[4,2,32,4096]{3,2,1,0:T(8,128)(2,1)} %air_ref.1) | copy-start | bytes 6291460
  2.2 11.3 %copy-start.3 = (bf16[2,32,4096]{2,1,0:T(8,128)(2,1)S(1)}, bf16[2,32,4096]{2,1,0:T(8,128)(2,1)}, u32[]{:S(2)}) copy-start(bf16[2,32,4096]{2,1,0:T(8,128)(2,1)} %kappa_ref.1) | copy-start | bytes 1572868
  2.7 10.8 %collective-permute-start = (bf16[4,2,4096]{2,1,0:T(2,128)(2,1)S(1)}, bf16[4,2,4096]{2,1,0:T(2,128)(2,1)S(1)}, u32[]{:S(2)}, u32[]{:S(2)}) collective-permute-start(bf16[4,2,4096]{2,1,0:T(2,128)(2,1)S(1)} %get-tuple-element.12), channel_id=1, source_target_pairs={{0,2},{2,4},{4,6},{6,8},{8,10},{10,12},{12,14},{14,16},{16,18},{18... | collective-permute-start | bytes 196616 | tf_op jit(solution)/shard_map/ppermute | solution.py:321
  5.2 8.3 %collective-permute-start.1 = (bf16[4,2,4096]{2,1,0:T(2,128)(2,1)S(1)}, bf16[4,2,4096]{2,1,0:T(2,128)(2,1)S(1)}, u32[]{:S(2)}, u32[]{:S(2)}) collective-permute-start(bf16[4,2,4096]{2,1,0:T(2,128)(2,1)S(1)} %get-tuple-element.13), channel_id=1, source_target_pairs={{2,0},{4,2},{6,4},{8,6},{10,8},{12,10},{14,12},{16,14},{18,16},{20... | collective-permute-start | bytes 196616 | tf_op jit(solution)/shard_map/ppermute | solution.py:320
  7.7 1.0 %copy-start.4 = (f32[4,160,128]{2,1,0:T(8,128)S(1)}, f32[4,160,128]{2,1,0:T(8,128)}, u32[]{:S(2)}) copy-start(f32[4,160,128]{2,1,0:T(8,128)} %constant.65.clone.base_cos) | copy-start | bytes 983044
  8.7 1.0 %copy-start.5 = (f32[4,160,128]{2,1,0:T(8,128)S(1)}, f32[4,160,128]{2,1,0:T(8,128)}, u32[]{:S(2)}) copy-start(f32[4,160,128]{2,1,0:T(8,128)} %constant.66.clone.base_sin) | copy-start | bytes 983044
  9.6 1.0 %copy-start.6 = (f32[4,160,128]{2,1,0:T(8,128)S(1)}, f32[4,160,128]{2,1,0:T(8,128)}, u32[]{:S(2)}) copy-start(f32[4,160,128]{2,1,0:T(8,128)} %constant.67.clone.step_cos) | copy-start | bytes 983044
  10.6 1.0 %copy-start.7 = (f32[4,160,128]{2,1,0:T(8,128)S(1)}, f32[4,160,128]{2,1,0:T(8,128)}, u32[]{:S(2)}) copy-start(f32[4,160,128]{2,1,0:T(8,128)} %constant.68.clone.step_sin) | copy-start | bytes 983044
  11.6 11.7 %copy-start = (bf16[32,320,641]{2,1,0:T(8,128)(2,1)S(1)}, bf16[32,320,641]{2,1,0:T(8,128)(2,1)}, u32[]{:S(2)}) copy-start(bf16[32,320,641]{2,1,0:T(8,128)(2,1)} %table_ref.5) | copy-start | bytes 39383044
  28.9 4.6 %collective-permute-start.10 = (bf16[168,8,128]{2,1,0:T(8,128)(2,1)S(1)}, bf16[168,8,128]{2,1,0:T(8,128)(2,1)S(1)}, u32[]{:S(2)}, u32[]{:S(2)}) collective-permute-start(bf16[168,8,128]{2,1,0:T(8,128)(2,1)S(1)} %get-tuple-element.21), channel_id=1, source_target_pairs={{0,2},{2,0},{4,6},{6,4},{8,10},{10,8},{12,14},{14,12},{16,18},{18,... | collective-permute-start | bytes 1032200 | tf_op jit(solution)/shard_map/ppermute | solution.py:352
  33.5 10.5 %collective-permute-start.11 = (bf16[84,8,128]{2,1,0:T(8,128)(2,1)S(1)}, bf16[84,8,128]{2,1,0:T(8,128)(2,1)S(1)}, u32[]{:S(2)}, u32[]{:S(2)}) collective-permute-start(bf16[84,8,128]{2,1,0:T(8,128)(2,1)S(1)} %add_convert_fusion.2), channel_id=1, source_target_pairs={{0,4},{2,6},{4,0},{6,2},{8,12},{10,14},{12,8},{14,10},{16,20},{18,... | collective-permute-start | bytes 516104 | tf_op jit(solution)/shard_map/ppermute | solution.py:352
  39.5 11.8 %collective-permute-start.6 = (bf16[160,8,256]{2,1,0:T(8,128)(2,1)S(1)}, bf16[160,8,256]{2,1,0:T(8,128)(2,1)S(1)}, u32[]{:S(2)}, u32[]{:S(2)}) collective-permute-start(bf16[160,8,256]{2,1,0:T(8,128)(2,1)S(1)} %get-tuple-element.19), channel_id=1, source_target_pairs={{0,2},{2,0},{4,6},{6,4},{8,10},{10,8},{12,14},{14,12},{16,18},{18,... | collective-permute-start | bytes 1966088 | tf_op jit(solution)/shard_map/ppermute | solution.py:352
  43.4 37.7 %copy-start.9 = (f32[4]{0:T(128)S(1)}, f32[4]{0:T(128)}, u32[]{:S(2)}) copy-start(f32[4]{0:T(128)} %param.11) | copy-start | bytes 52
  43.4 10.1 %collective-permute-start.2 = (bf16[160,8,256]{2,1,0:T(8,128)(2,1)S(1)}, bf16[160,8,256]{2,1,0:T(8,128)(2,1)S(1)}, u32[]{:S(2)}, u32[]{:S(2)}) collective-permute-start(bf16[160,8,256]{2,1,0:T(8,128)(2,1)S(1)} %get-tuple-element.17), channel_id=1, source_target_pairs={{0,2},{2,0},{4,6},{6,4},{8,10},{10,8},{12,14},{14,12},{16,18},{18,... | collective-permute-start | bytes 1966088 | tf_op jit(solution)/shard_map/ppermute | solution.py:352
  44.1 4.6 %collective-permute-start.12 = (bf16[42,8,128]{2,1,0:T(8,128)(2,1)S(1)}, bf16[42,8,128]{2,1,0:T(8,128)(2,1)S(1)}, u32[]{:S(2)}, u32[]{:S(2)}) collective-permute-start(bf16[42,8,128]{2,1,0:T(8,128)(2,1)S(1)} %add_convert_fusion.5), channel_id=1, source_target_pairs={{0,8},{2,10},{4,12},{6,14},{8,0},{10,2},{12,4},{14,6},{16,24},{18,... | collective-permute-start | bytes 258056 | tf_op jit(solution)/shard_map/ppermute | solution.py:352
  48.6 6.3 %collective-permute-start.13 = (bf16[21,8,128]{2,1,0:T(8,128)(2,1)S(1)}, bf16[21,8,128]{2,1,0:T(8,128)(2,1)S(1)}, u32[]{:S(2)}, u32[]{:S(2)}) collective-permute-start(bf16[21,8,128]{2,1,0:T(8,128)(2,1)S(1)} %add_convert_fusion.8), channel_id=1, source_target_pairs={{0,16},{2,18},{4,20},{6,22},{8,24},{10,26},{12,28},{14,30},{16,0},... | collective-permute-start | bytes 129032 | tf_op jit(solution)/shard_map/ppermute | solution.py:352
  52.1 10.8 %collective-permute-start.7 = (bf16[80,8,256]{2,1,0:T(8,128)(2,1)}, bf16[80,8,256]{2,1,0:T(8,128)(2,1)S(1)}, u32[]{:S(2)}, u32[]{:S(2)}) collective-permute-start(bf16[80,8,256]{2,1,0:T(8,128)(2,1)} %add_convert_fusion), channel_id=1, source_target_pairs={{0,4},{2,6},{4,0},{6,2},{8,12},{10,14},{12,8},{14,10},{16,20},{18,... | collective-permute-start | bytes 983048 | tf_op jit(solution)/shard_map/ppermute | solution.py:352
  54.3 13.2 %collective-permute-start.3 = (bf16[80,8,256]{2,1,0:T(8,128)(2,1)}, bf16[80,8,256]{2,1,0:T(8,128)(2,1)S(1)}, u32[]{:S(2)}, u32[]{:S(2)}) collective-permute-start(bf16[80,8,256]{2,1,0:T(8,128)(2,1)} %add_convert_fusion.1), channel_id=1, source_target_pairs={{0,4},{2,6},{4,0},{6,2},{8,12},{10,14},{12,8},{14,10},{16,20},{18,... | collective-permute-start | bytes 983048 | tf_op jit(solution)/shard_map/ppermute | solution.py:352
  63.0 6.3 %collective-permute-start.8 = (bf16[40,8,256]{2,1,0:T(8,128)(2,1)S(1)}, bf16[40,8,256]{2,1,0:T(8,128)(2,1)S(1)}, u32[]{:S(2)}, u32[]{:S(2)}) collective-permute-start(bf16[40,8,256]{2,1,0:T(8,128)(2,1)S(1)} %add_convert_fusion.3), channel_id=1, source_target_pairs={{0,8},{2,10},{4,12},{6,14},{8,0},{10,2},{12,4},{14,6},{16,24},{18,... | collective-permute-start | bytes 491528 | tf_op jit(solution)/shard_map/ppermute | solution.py:352
  67.6 6.1 %collective-permute-start.4 = (bf16[40,8,256]{2,1,0:T(8,128)(2,1)S(1)}, bf16[40,8,256]{2,1,0:T(8,128)(2,1)S(1)}, u32[]{:S(2)}, u32[]{:S(2)}) collective-permute-start(bf16[40,8,256]{2,1,0:T(8,128)(2,1)S(1)} %add_convert_fusion.4), channel_id=1, source_target_pairs={{0,8},{2,10},{4,12},{6,14},{8,0},{10,2},{12,4},{14,6},{16,24},{18,... | collective-permute-start | bytes 491528 | tf_op jit(solution)/shard_map/ppermute | solution.py:352
  69.3 7.6 %collective-permute-start.9 = (bf16[20,8,256]{2,1,0:T(8,128)(2,1)S(1)}, bf16[20,8,256]{2,1,0:T(8,128)(2,1)S(1)}, u32[]{:S(2)}, u32[]{:S(2)}) collective-permute-start(bf16[20,8,256]{2,1,0:T(8,128)(2,1)S(1)} %add_convert_fusion.6), channel_id=1, source_target_pairs={{0,16},{2,18},{4,20},{6,22},{8,24},{10,26},{12,28},{14,30},{16,0},... | collective-permute-start | bytes 245768 | tf_op jit(solution)/shard_map/ppermute | solution.py:352
  73.7 3.2 %copy-start.8 = (bf16[40,8,256]{2,1,0:T(8,128)(2,1)}, bf16[40,8,256]{2,1,0:T(8,128)(2,1)S(1)}, u32[]{:S(2)}) copy-start(bf16[40,8,256]{2,1,0:T(8,128)(2,1)S(1)} %collective-permute-done.4) | copy-start | bytes 491524
  74.4 5.7 %collective-permute-start.5 = (bf16[20,8,256]{2,1,0:T(8,128)(2,1)}, bf16[20,8,256]{2,1,0:T(8,128)(2,1)}, u32[]{:S(2)}, u32[]{:S(2)}) collective-permute-start(bf16[20,8,256]{2,1,0:T(8,128)(2,1)} %add_convert_fusion.7), channel_id=1, source_target_pairs={{0,16},{2,18},{4,20},{6,22},{8,24},{10,26},{12,28},{14,30},{16,0},... | collective-permute-start | bytes 245768 | tf_op jit(solution)/shard_map/ppermute | solution.py:352
  82.5 6.8 %collective-permute-start.14 = (f32[20,2,641]{2,1,0:T(2,128)S(1)}, f32[20,2,641]{2,1,0:T(2,128)S(1)}, u32[]{:S(2)}, u32[]{:S(2)}) collective-permute-start(f32[20,2,641]{2,1,0:T(2,128)S(1)} %get-tuple-element.24), channel_id=1, source_target_pairs={{1,0},{3,2},{5,4},{7,6},{9,8},{11,10},{13,12},{15,14},{17,16},{19,... | collective-permute-start | bytes 307688 | tf_op jit(solution)/shard_map/ppermute | solution.py:369

commit v3 on v2

--- a/solution.py
+++ b/solution.py
@@ -36,9 +36,8 @@
     )(air, air)
 
 
-def wave_kernel(base_cos, base_sin, step_cos, step_sin, out_ref):
-    cos, sin = base_cos[0], base_sin[0]
-    turn_cos, turn_sin = step_cos[0], step_sin[0]
+def wave_kernel(table_ref, out_ref):
+    cos, sin, turn_cos, turn_sin = (table_ref[0, kind] for kind in range(4))
     lanes = cos.shape[-1]
     for block in range(out_ref.shape[-1] // lanes):
         at = slice(block * lanes, (block + 1) * lanes)
@@ -61,15 +60,13 @@
             turn.append(phase * (2.0 * math.pi / lon))
     base, turn = np.stack(base), np.stack(turn)
     scale = 1.0 / math.sqrt(lon)
-    tables = [
-        jnp.asarray(table, jnp.float32)
-        for table in (np.cos(base) * scale, -np.sin(base) * scale, np.cos(turn), -np.sin(turn))
-    ]
-    spec = pl.BlockSpec((1, count // 2, lanes), lambda i, j: (i, j, 0))
+    tables = np.stack(
+        [np.cos(base) * scale, -np.sin(base) * scale, np.cos(turn), -np.sin(turn)], axis=1
+    )
     return pl.pallas_call(
         wave_kernel,
         grid=(4, 2),
-        in_specs=[spec] * 4,
+        in_specs=[pl.BlockSpec((1, 4, count // 2, lanes), lambda i, j: (i, 0, j, 0))],
         out_specs=pl.BlockSpec((1, 2, count // 2, half), lambda i, j: (i, 0, j, 0)),
         out_shape=jax.ShapeDtypeStruct((4, 2, count, half), jnp.bfloat16),
         compiler_params=pltpu.CompilerParams(vmem_limit_bytes=8 << 20),
@@ -77,7 +74,7 @@
             flops=4 * 2 * count * half * 3, bytes_accessed=4 * 2 * count * half * 2, transcendentals=0
         ),
         name="waves",
-    )(*tables)
+    )(jnp.asarray(tables, jnp.float32))
 
 
 def smooth_kernel(
@@ -214,97 +211,98 @@
 
 
 def legendre_kernel(
-    half_k, start, extra, place_ref, block_ref, table_ref, keep_ref, send_ref, spectra, turned, sems
+    half_k, start, extra, place_ref, chunk_ref, within_ref, block_ref, table_ref, keep_ref, send_ref,
+    spectra, turned, spare, sems
 ):
-    step = pl.program_id(0)
-    rows, pairs, width = table_ref.shape
-    groups = pairs // GROUP
+    rows = table_ref.shape[0]
+    groups = turned.shape[0]
+    width = turned.shape[1] * LANES
+    columns = min(width, 2 * half_k + 1 - start)
     _, channels, kept = spectra.shape
-    slots = place_ref[half_k]
     lane = lax.broadcasted_iota(jnp.int32, (channels, LANES), 1)
-    for group in range(groups):
-        table = table_ref[:, group * GROUP : (group + 1) * GROUP, :].reshape(rows * GROUP, width)
-        left = block_ref[group].reshape(4 * channels * GROUP, rows * GROUP)
-        sums = jnp.dot(left, table, preferred_element_type=jnp.float32)
-        sums = sums.reshape(2, 2, channels, GROUP, width)
-        first_pair = (step * groups + group) * GROUP
-        pair = first_pair + lax.broadcasted_iota(jnp.int32, (GROUP, width), 0)
-        column = start + lax.broadcasted_iota(jnp.int32, (GROUP, width), 1)
-        first = column < 2 * half_k - pair
-        odd = jnp.where(first, column, column - 2 * half_k + pair) & 1
-        even = (odd == 0)[None]
-        chosen = jnp.where(
-            first[None],
-            jnp.where(even, sums[0, 0], sums[0, 1]),
-            jnp.where(even, sums[1, 0], sums[1, 1]),
-        )
-        chosen = chosen.reshape(channels * GROUP, width)
-        for tile in range(width // LANES):
-            turned[group, tile] = chosen[:, tile * LANES : (tile + 1) * LANES]
-        for member in range(GROUP):
-            place = place_ref[first_pair + member]
-            for tile in range(kept // LANES):
-                value = turned[group, tile, pl.ds(member, channels, stride=GROUP), :]
-                spectra[place, :, tile * LANES : (tile + 1) * LANES] = value.astype(spectra.dtype)
-            if extra:
-                chunk = place // (slots + 1)
-                within = place - chunk * (slots + 1)
-                spare = chunk * (slots + 1) + slots
-                value = turned[group, kept // LANES, pl.ds(member, channels, stride=GROUP), :]
-                value = jnp.broadcast_to(value[:, :1], (channels, LANES)).astype(spectra.dtype)
-                before = spectra[spare, :, :LANES]
-                spectra[spare, :, :LANES] = jnp.where(lane == within, value, before)
-
-    @pl.when(step == pl.num_programs(0) - 1)
-    def _():
-        count = spectra.shape[0] // 2
-        send = pltpu.make_async_copy(spectra.at[pl.ds(count, count)], send_ref, sems.at[0])
-        keep = pltpu.make_async_copy(spectra.at[pl.ds(0, count)], keep_ref, sems.at[1])
-        send.start()
-        keep.start()
-        send.wait()
-        keep.wait()
-
-
-def legendre(places, blocks, table, start, kept, extra, total):
+    def trip(step, carry):
+        for group in range(groups):
+            first_pair = pl.multiple_of((step * groups + group) * GROUP, GROUP)
+            table = table_ref[:, pl.ds(first_pair, GROUP), start : start + columns]
+            table = table.reshape(rows * GROUP, columns)
+            left = block_ref[step * groups + group].reshape(4 * channels * GROUP, rows * GROUP)
+            sums = jnp.dot(left, table, preferred_element_type=jnp.float32)
+            sums = sums.reshape(2, 2, channels, GROUP, columns)
+            pair = first_pair + lax.broadcasted_iota(jnp.int32, (GROUP, columns), 0)
+            column = start + lax.broadcasted_iota(jnp.int32, (GROUP, columns), 1)
+            first = column < 2 * half_k - pair
+            odd = jnp.where(first, column, column - 2 * half_k + pair) & 1
+            even = (odd == 0)[None]
+            chosen = jnp.where(
+                first[None],
+                jnp.where(even, sums[0, 0], sums[0, 1]),
+                jnp.where(even, sums[1, 0], sums[1, 1]),
+            )
+            chosen = chosen.reshape(channels * GROUP, columns)
+            for tile in range(width // LANES):
+                part = chosen[:, tile * LANES : (tile + 1) * LANES]
+                turned[group, tile, :, : part.shape[1]] = part
+            for member in range(GROUP):
+                place = place_ref[first_pair + member]
+                for tile in range(kept // LANES):
+                    value = turned[group, tile, pl.ds(member, channels, stride=GROUP), :]
+                    spectra[place, :, tile * LANES : (tile + 1) * LANES] = value.astype(spectra.dtype)
+                if extra:
+                    chunk = chunk_ref[first_pair + member]
+                    within = within_ref[first_pair + member]
+                    value = turned[group, kept // LANES, pl.ds(member, channels, stride=GROUP), :]
+                    value = jnp.broadcast_to(value[:, :1], (channels, LANES))
+                    pltpu.store(spare.at[chunk], value, mask=lane == within)
+        return carry
+
+    lax.fori_loop(0, half_k // (groups * GROUP), trip, 0)
+    if extra:
+        stride = spectra.shape[0] // spare.shape[0]
+        for chunk in range(spare.shape[0]):
+            spectra[(chunk + 1) * stride - 1, :, :LANES] = spare[chunk].astype(spectra.dtype)
+    count = spectra.shape[0] // 2
+    send = pltpu.make_async_copy(spectra.at[pl.ds(count, count)], send_ref, sems.at[0])
+    keep = pltpu.make_async_copy(spectra.at[pl.ds(0, count)], keep_ref, sems.at[1])
+    send.start()
+    keep.start()
+    send.wait()
+    keep.wait()
+
+
+def legendre(places, blocks, table, start, kept, extra, bands, stride):
     rows, half_k, _ = table.shape
     channels = blocks.shape[1] * blocks.shape[2] // (4 * GROUP)
     pairs = 8 * GROUP
     groups = pairs // GROUP
     width = kept + (LANES if extra else 0)
+    total = bands * stride
     result = jax.ShapeDtypeStruct((total // 2, channels, kept), jnp.bfloat16)
     return pl.pallas_call(
         functools.partial(legendre_kernel, half_k, start, extra),
         grid_spec=pltpu.PrefetchScalarGridSpec(
-            num_scalar_prefetch=1,
-            grid=(half_k // pairs,),
-            in_specs=[
-                pl.BlockSpec((groups, *blocks.shape[1:]), lambda i, s: (i, 0, 0, 0)),
-                pl.BlockSpec((rows, pairs, width), lambda i, s: (0, i, start // width)),
-            ],
+            num_scalar_prefetch=3,
+            in_specs=[pl.BlockSpec(memory_space=pltpu.VMEM)] * 2,
             out_specs=[pl.BlockSpec(memory_space=pl.ANY)] * 2,
             scratch_shapes=[
                 pltpu.VMEM((total, channels, kept), jnp.bfloat16),
                 pltpu.VMEM((groups, width // LANES, channels * GROUP, LANES), jnp.float32),
+                pltpu.VMEM((bands, channels, LANES), jnp.float32),
                 pltpu.SemaphoreType.DMA((2,)),
             ],
         ),
         out_shape=[result, result],
-        compiler_params=pltpu.CompilerParams(vmem_limit_bytes=24 << 20),
+        compiler_params=pltpu.CompilerParams(vmem_limit_bytes=8 << 20),
         cost_estimate=pl.CostEstimate(
             flops=2 * blocks.size * width,
             bytes_accessed=2 * (blocks.size + rows * half_k * width),
             transcendentals=0,
         ),
         name="legendre",
-    )(places, blocks, table)
-
-
-def reversed_bits(value, bits):
-    result = jnp.zeros_like(value)
-    for bit in range(bits):
-        result = result * 2 + ((value >> bit) & 1)
-    return result
+    )(
+        *places,
+        pltpu.with_memory_space_constraint(blocks, pltpu.VMEM),
+        pltpu.with_memory_space_constraint(table, pltpu.VMEM),
+    )
 
 
 def on_device(air, kappa, depth, table, mode_degree):
@@ -328,36 +326,68 @@
     is_last = (band == bands - 1).astype(jnp.int32)[None]
     slot = jnp.arange(half_k, dtype=jnp.int32)
     here = mode_degree[None, :] == slot[:, None]
-    chunk = reversed_bits((slot // slots) ^ band, bits)
-
-    def places_with(stride):
-        place = chunk * stride + slot % slots
-        found = jnp.sum(jnp.where(here, place[None, :], 0), axis=1, dtype=jnp.int32)
-        return jnp.concatenate([found, jnp.full((1,), slots, jnp.int32)])
+    relative = (slot // slots) ^ band
+
+    def places_with(order, stride):
+        chunk = sum(((relative >> bit) & 1) << (bits - 1 - at) for at, bit in enumerate(order))
+        within = slot % slots
+        return [
+            jnp.sum(jnp.where(here, value[None, :], 0), axis=1, dtype=jnp.int32)
+            for value in (chunk * stride + within, chunk, within)
+        ]
 
     smoothed, folds = smooth(air, kappa, above, below, up, down, is_last)
     blocks = fourier_blocks(waves, folds.reshape(2, 2 * levels * rows, lon // 2), rows)
-    pieces = []
+    natural = list(range(bits))
+    crossed = natural if bits < 3 else [0, 2, 1, *range(3, bits)]
     top = columns - 1
-    for start in range(0, top, WIDTH):
+    streams = []
+    for index, start in enumerate(range(0, top, WIDTH)):
         kept = min(WIDTH, top - start)
         extra = start + kept == top
         stride = slots + 1 if extra else slots
-        keep, count = legendre(
-            places_with(stride), blocks, table, start, kept, extra, stride * bands
-        ), stride * bands // 2
-        held, outgoing = [keep[0]], keep[1]
-        for bit in range(bits):
-            held.append(
-                lax.ppermute(outgoing, "band", [(i, i ^ (1 << bit)) for i in range(bands)])
-            )
-            count //= 2
-            if bit < bits - 1:
-                outgoing = sum(part[count : 2 * count].astype(jnp.float32) for part in held)
-                outgoing = outgoing.astype(jnp.bfloat16)
-        done = sum(part[:stride].astype(jnp.float32) for part in held)
+        order = crossed if index == 1 else natural
+        streams.append(dict(start=start, kept=kept, extra=extra, stride=stride, order=order))
+
+    def outgoing_of(stream):
+        count = stream["outgoing"].shape[0] // 2 if "outgoing" in stream else None
+        parts = [part[count : 2 * count].astype(jnp.float32) for part in stream["held"]]
+        return sum(parts).astype(jnp.bfloat16)
+
+    def send(stream, at, outgoing):
+        bit = stream["order"][at]
+        stream["outgoing"] = outgoing
+        stream["held"].append(
+            lax.ppermute(outgoing, "band", [(i, i ^ (1 << bit)) for i in range(bands)])
+        )
+
+    previous = None
+    for index, stream in enumerate(streams):
+        where = places_with(stream["order"], stream["stride"])
+        if previous is not None:
+            where = lax.optimization_barrier((where, previous))[0]
+        keep, outgoing = legendre(
+            where, blocks, table, stream["start"], stream["kept"], stream["extra"], bands,
+            stream["stride"],
+        )
+        stream["held"] = [keep]
+        send(stream, 0, outgoing)
+        previous = [keep]
+        if index > 0 and bits > 1:
+            earlier = streams[index - 1]
+            crossing = outgoing_of(earlier)
+            send(earlier, 1, crossing)
+            previous.append(crossing)
+    if bits > 1:
+        send(streams[-1], 1, outgoing_of(streams[-1]))
+    for at in range(2, bits):
+        for stream in streams:
+            send(stream, at, outgoing_of(stream))
+    pieces = []
+    for stream in streams:
+        done = sum(part[: stream["stride"]].astype(jnp.float32) for part in stream["held"])
         pieces.append(done[:slots])
-        if extra:
+        if stream["extra"]:
             pieces.append(jnp.swapaxes(done[slots, :, :slots], 0, 1)[:, :, None])
     mine = jnp.concatenate(pieces, axis=2)
     mine = mine.reshape(slots, levels, 2, columns)

time: 91.6 us -> 76.1 us (0.83)
  waiting for transfers between devices: 28.9 us -> 14.4 us
  starting transfers between devices: 21.1 us -> 27.4 us
  local copies, waits for them, and re-layouts: 6.76 us -> 3.64 us
  other arithmetic: 8.11 us -> 5.62 us
  Pallas kernels: 25.4 us -> 23.8 us
    ppermute x12, waiting for transfers between devices: 23.7 us -> 9.31 us  [send(): lax.ppermute(outgoing, 'band', [(i, i ^ 1 << bit) for i in range(bands)])]
    ppermute x12, starting transfers between devices: 16 us -> 22.5 us  [send(): lax.ppermute(outgoing, 'band', [(i, i ^ 1 << bit) for i in range(bands)])]
    unnamed x20 -> x12, local copies, waits for them, and re-layouts: 5.49 us -> 2.98 us
    pallas_call x3, Pallas kernels: 13.4 us -> 11 us  [legendre(): pl.pallas_call(functools.partial(legendre_kernel, half_k, start, extra),...]
    convert_element_type x9, other arithmetic: 2.59 us -> 0.49 us  [outgoing_of(): return sum(parts).astype(jnp.bfloat16)]
    reduce_sum x1, other arithmetic: 0.92 us -> 1.92 us  [places_with(): jnp.sum(jnp.where(here, value[None, :], 0), axis=1, dtype=jnp.int32)]
    reduce_sum x1, other arithmetic: 1.33 us -> 0.39 us  [on_device(): total = jnp.sum(weighted, axis=1)]
  transfers between devices with their start and end apart: 15 -> 15, of which waited for: 8 -> 7; matrix products, arithmetic and copies ran while one was open for 6% -> 5% of each run, Pallas kernels for 11% -> 12%
where the time goes in v3:
time: 76.1 us; the launch traced here: 75.8 us
  starting transfers between devices  27.4 us (36%)
  Pallas kernels  23.8 us (31%)
  waiting for transfers between devices  14.4 us (19%)
  other arithmetic  5.62 us (7%)
  local copies, waits for them, and re-layouts  3.64 us (5%)
  between operations  0.88 us (1%)
    ppermute x12, starting transfers between devices, send(): lax.ppermute(outgoing, 'band', [(i, i ^ 1 << bit) for i in range(bands)])  22.5 us
    pallas_call x3, Pallas kernels, legendre(): pl.pallas_call(functools.partial(legendre_kernel, half_k, start, extra),...  11 us
    ppermute x12, waiting for transfers between devices, send(): lax.ppermute(outgoing, 'band', [(i, i ^ 1 << bit) for i in range(bands)])  9.31 us
    pallas_call x1, Pallas kernels, smooth(): pl.pallas_call(smooth_kernel, grid=(levels,), in_specs=[pl.BlockSpec(memo...  5.87 us
    ppermute x1, waiting for transfers between devices, on_device(): lower = lax.ppermute(total, 'lev', [(i + 1, i) for i in range(levs - 1)])  5.13 us
    pallas_call x1, Pallas kernels, fourier_blocks(): pl.pallas_call(functools.partial(fourier_kernel, rows), grid=(2,), in_spe...  3.84 us
    unnamed x12, local copies, waits for them, and re-layouts  2.98 us
    ppermute x1, starting transfers between devices, on_device(): above = lax.ppermute(tail, 'band', [(i, i + 1) for i in range(bands - 1)])  2.39 us
  transfers between devices with their start and end apart: 15, of which 7 were waited for; matrix products, arithmetic and copies ran while one was open for 5% of the time, Pallas kernels for 12%

profile of v3, /device:TPU:0, one launch (start us, length us, event | category | flops | bytes accessed | tf_op | source)
XLA Modules:
  0.0 75.8 jit_solution(643202620190432242)
XLA Ops:
  0.6 1.6 %copy-done.1 = bf16[4,2,32,4096]{3,2,1,0:T(8,128)(2,1)S(1)} copy-done((bf16[4,2,32,4096]{3,2,1,0:T(8,128)(2,1)S(1)}, bf16[4,2,32,4096]{3,2,1,0:T(8,128)(2,1)}, u32[]{:S(2)}) %copy-start.1) | copy-done | bytes 2097176
  2.2 1.1 %edges.1 = (bf16[4,2,4096]{2,1,0:T(2,128)(2,1)}, bf16[4,2,4096]{2,1,0:T(2,128)(2,1)}) custom-call(bf16[4,2,32,4096]{3,2,1,0:T(8,128)(2,1)S(1)} %copy-done.1, bf16[4,2,32,4096]{3,2,1,0:T(8,128)(2,1)S(1)} %copy-done.1), custom_call_target="tpu_custom_call" | custom-call | tf_op jit(solution)/shard_map/edges/pallas_call | solution.py:25
  3.3 2.4 %collective-permute-start = (bf16[4,2,4096]{2,1,0:T(2,128)(2,1)}, bf16[4,2,4096]{2,1,0:T(2,128)(2,1)S(1)}, u32[]{:S(2)}, u32[]{:S(2)}) collective-permute-start(bf16[4,2,4096]{2,1,0:T(2,128)(2,1)} %get-tuple-element.18), channel_id=1, source_target_pairs={{0,2},{2,4},{4,6},{6,8},{8,10},{10,12},{12,14},{14,16},{16,18},{18... | collective-permute-start | bytes 196616 | tf_op jit(solution)/shard_map/ppermute | solution.py:319
  5.7 1.3 %collective-permute-start.1 = (bf16[4,2,4096]{2,1,0:T(2,128)(2,1)}, bf16[4,2,4096]{2,1,0:T(2,128)(2,1)S(1)}, u32[]{:S(2)}, u32[]{:S(2)}) collective-permute-start(bf16[4,2,4096]{2,1,0:T(2,128)(2,1)} %get-tuple-element.19), channel_id=1, source_target_pairs={{2,0},{4,2},{6,4},{8,6},{10,8},{12,10},{14,12},{16,14},{18,16},{20... | collective-permute-start | bytes 196616 | tf_op jit(solution)/shard_map/ppermute | solution.py:318
  7.1 0.6 add_add_fusion
  7.7 2.0 %waves.1.wave_ref = bf16[4,2,160,2048]{3,2,1,0:T(8,128)(2,1)S(1)} custom-call(f32[4,4,160,128]{3,2,1,0:T(8,128)S(1)} %copy-done.3), custom_call_target="tpu_custom_call" | custom-call | flops 7864320 | bytes 5242880 | tf_op jit(solution)/shard_map/waves/pallas_call | solution.py:66
  9.7 1.9 %select_reduce_fusion.5 = (s32[320]{0:T(512)S(1)}, s32[320]{0:T(512)S(1)}, s32[320]{0:T(512)S(1)}, s32[320]{0:T(512)S(1)}, s32[320]{0:T(512)S(1)}, /*index=5*/s32[320]{0:T(512)S(1)}) fusion(s32[320]{0:T(512)} %get-tuple-element.49, s32[320]{0:T(512)} %param.10, s32[320]{0:T(512)S(1)} %get-tuple-element.46, s32[320]{0:T(512)} %get-tuple-element.48, ...), kind=kLoop, calls=%fused_computation.10 | loop fusion | flops 1329280 | bytes 16640 | tf_op jit(solution)/shard_map/reduce_sum | solution.py:335
  11.8 1.4 %copy-done.4 = bf16[2,32,4096]{2,1,0:T(8,128)(2,1)S(1)} copy-done((bf16[2,32,4096]{2,1,0:T(8,128)(2,1)S(1)}, bf16[2,32,4096]{2,1,0:T(8,128)(2,1)}, u32[]{:S(2)}) %copy-start.4) | copy-done | bytes 524312
  13.2 5.9 %smooth.1 = (bf16[4,2,32,4096]{3,2,1,0:T(8,128)(2,1)}, bf16[2,2,4,32,2048]{4,3,2,1,0:T(8,128)(2,1)S(1)}) custom-call(s32[1]{0:T(128)} %bitcast.last_ref, bf16[4,2,32,4096]{3,2,1,0:T(8,128)(2,1)S(1)} %copy-done.2, bf16[2,32,4096]{2,1,0:T(8,128)(2,1)S(1)} %copy-done.4, bf16[4,2,4096]{2,1,0:T(2,128)(2,1)S(1)} %collective-permute-done.above_ref, ...), custom_call_target="tpu_custom_call" | custom-call | flops 20971520 | bytes 7340032 | tf_op jit(solution)/shard_map/smooth/pallas_call | solution.py:118
  19.1 3.8 %fourier.1.block_ref = bf16[40,2,128,256]{3,2,1,0:T(8,128)(2,1)S(1)} custom-call(bf16[4,2,160,2048]{3,2,1,0:T(8,128)(2,1)S(1)} %waves.1.wave_ref, bf16[2,256,2048]{2,1,0:T(8,128)(2,1)S(1)} %bitcast.57), custom_call_target="tpu_custom_call" | custom-call | flops 1342177280 | bytes 7340032 | tf_op jit(solution)/shard_map/fourier/pallas_call | solution.py:193
  22.9 3.6 %legendre.3 = (bf16[160,8,256]{2,1,0:T(8,128)(2,1)S(1)}, bf16[160,8,256]{2,1,0:T(8,128)(2,1)S(1)}) custom-call(s32[320]{0:T(512)S(1)} %get-tuple-element.34.place_ref, s32[320]{0:T(512)S(1)} %get-tuple-element.30.chunk_ref, s32[320]{0:T(512)S(1)} %get-tuple-element.31.within_ref, bf16[40,2,128,256]{3,2,1,0:T(8,128)(2,1)S(1)} %fourier.1.block_ref, ...), custom_call_target="tpu_custom_call" | custom-call | flops 1342177280 | bytes 10485760 | tf_op jit(solution)/shard_map/legendre/pallas_call | solution.py:280
  26.6 3.3 %collective-permute-start.2 = (bf16[160,8,256]{2,1,0:T(8,128)(2,1)S(1)}, bf16[160,8,256]{2,1,0:T(8,128)(2,1)S(1)}, u32[]{:S(2)}, u32[]{:S(2)}) collective-permute-start(bf16[160,8,256]{2,1,0:T(8,128)(2,1)S(1)} %get-tuple-element.23), channel_id=1, source_target_pairs={{0,2},{2,0},{4,6},{6,4},{8,10},{10,8},{12,14},{14,12},{16,18},{18,... | collective-permute-start | bytes 1966088 | tf_op jit(solution)/shard_map/ppermute | solution.py:361
  29.9 3.6 %legendre.4 = (bf16[160,8,256]{2,1,0:T(8,128)(2,1)S(1)}, bf16[160,8,256]{2,1,0:T(8,128)(2,1)S(1)}) custom-call(s32[320]{0:T(512)S(1)} %get-tuple-element.24.place_ref, s32[320]{0:T(512)S(1)} %get-tuple-element.25.chunk_ref, s32[320]{0:T(512)S(1)} %get-tuple-element.31.within_ref, bf16[40,2,128,256]{3,2,1,0:T(8,128)(2,1)S(1)} %fourier.1.block_ref, ...), custom_call_target="tpu_custom_call" | custom-call | flops 1342177280 | bytes 10485760 | tf_op jit(solution)/shard_map/legendre/pallas_call | solution.py:280
  33.6 2.2 %collective-permute-start.3 = (bf16[80,8,256]{2,1,0:T(8,128)(2,1)S(1)}, bf16[80,8,256]{2,1,0:T(8,128)(2,1)S(1)}, u32[]{:S(2)}, u32[]{:S(2)}) collective-permute-start(bf16[80,8,256]{2,1,0:T(8,128)(2,1)S(1)} %add_convert_fusion.1), channel_id=1, source_target_pairs={{0,4},{2,6},{4,0},{6,2},{8,12},{10,14},{12,8},{14,10},{16,20},{18,... | collective-permute-start | bytes 983048 | tf_op jit(solution)/shard_map/ppermute | solution.py:361
  35.9 2.6 %collective-permute-start.7 = (bf16[80,8,256]{2,1,0:T(8,128)(2,1)S(1)}, bf16[80,8,256]{2,1,0:T(8,128)(2,1)S(1)}, u32[]{:S(2)}, u32[]{:S(2)}) collective-permute-start(bf16[80,8,256]{2,1,0:T(8,128)(2,1)S(1)} %add_convert_fusion), channel_id=1, source_target_pairs={{0,8},{2,10},{4,12},{6,14},{8,0},{10,2},{12,4},{14,6},{16,24},{18,... | collective-permute-start | bytes 983048 | tf_op jit(solution)/shard_map/ppermute | solution.py:361
  38.5 3.8 %legendre.5 = (bf16[168,8,128]{2,1,0:T(8,128)(2,1)S(1)}, bf16[168,8,128]{2,1,0:T(8,128)(2,1)S(1)}) custom-call(s32[320]{0:T(512)S(1)} %get-tuple-element.29.place_ref, s32[320]{0:T(512)S(1)} %get-tuple-element.30.chunk_ref, s32[320]{0:T(512)S(1)} %get-tuple-element.31.within_ref, bf16[40,2,128,256]{3,2,1,0:T(8,128)(2,1)S(1)} %fourier.1.block_ref, ...), custom_call_target="tpu_custom_call" | custom-call | flops 1342177280 | bytes 10485760 | tf_op jit(solution)/shard_map/legendre/pallas_call | solution.py:280
  42.5 1.3 %collective-permute-done.3 = bf16[80,8,256]{2,1,0:T(8,128)(2,1)S(1)} collective-permute-done((bf16[80,8,256]{2,1,0:T(8,128)(2,1)S(1)}, bf16[80,8,256]{2,1,0:T(8,128)(2,1)S(1)}, u32[]{:S(2)}, u32[]{:S(2)}) %collective-permute-start.3) | collective-permute-done | bytes 327712 | tf_op jit(solution)/shard_map/ppermute | solution.py:361
  43.8 2.7 %collective-permute-start.4 = (bf16[40,8,256]{2,1,0:T(8,128)(2,1)S(1)}, bf16[40,8,256]{2,1,0:T(8,128)(2,1)S(1)}, u32[]{:S(2)}, u32[]{:S(2)}) collective-permute-start(bf16[40,8,256]{2,1,0:T(8,128)(2,1)S(1)} %add_convert_fusion.4), channel_id=1, source_target_pairs={{0,8},{2,10},{4,12},{6,14},{8,0},{10,2},{12,4},{14,6},{16,24},{18,... | collective-permute-start | bytes 491528 | tf_op jit(solution)/shard_map/ppermute | solution.py:361
  47.0 0.8 %collective-permute-start.8 = (bf16[40,8,256]{2,1,0:T(8,128)(2,1)S(1)}, bf16[40,8,256]{2,1,0:T(8,128)(2,1)S(1)}, u32[]{:S(2)}, u32[]{:S(2)}) collective-permute-start(bf16[40,8,256]{2,1,0:T(8,128)(2,1)S(1)} %add_convert_fusion.3), channel_id=1, source_target_pairs={{0,4},{2,6},{4,0},{6,2},{8,12},{10,14},{12,8},{14,10},{16,20},{18,... | collective-permute-start | bytes 491528 | tf_op jit(solution)/shard_map/ppermute | solution.py:361
  47.8 1.3 %collective-permute-start.11 = (bf16[84,8,128]{2,1,0:T(8,128)(2,1)S(1)}, bf16[84,8,128]{2,1,0:T(8,128)(2,1)S(1)}, u32[]{:S(2)}, u32[]{:S(2)}) collective-permute-start(bf16[84,8,128]{2,1,0:T(8,128)(2,1)S(1)} %add_convert_fusion.2), channel_id=1, source_target_pairs={{0,4},{2,6},{4,0},{6,2},{8,12},{10,14},{12,8},{14,10},{16,20},{18,... | collective-permute-start | bytes 516104 | tf_op jit(solution)/shard_map/ppermute | solution.py:361
  49.2 1.1 %collective-permute-done.4 = bf16[40,8,256]{2,1,0:T(8,128)(2,1)S(1)} collective-permute-done((bf16[40,8,256]{2,1,0:T(8,128)(2,1)S(1)}, bf16[40,8,256]{2,1,0:T(8,128)(2,1)S(1)}, u32[]{:S(2)}, u32[]{:S(2)}) %collective-permute-start.4) | collective-permute-done | bytes 163872 | tf_op jit(solution)/shard_map/ppermute | solution.py:361
  50.3 2.8 %collective-permute-start.5 = (bf16[20,8,256]{2,1,0:T(8,128)(2,1)S(1)}, bf16[20,8,256]{2,1,0:T(8,128)(2,1)S(1)}, u32[]{:S(2)}, u32[]{:S(2)}) collective-permute-start(bf16[20,8,256]{2,1,0:T(8,128)(2,1)S(1)} %add_convert_fusion.7), channel_id=1, source_target_pairs={{0,16},{2,18},{4,20},{6,22},{8,24},{10,26},{12,28},{14,30},{16,0},... | collective-permute-start | bytes 245768 | tf_op jit(solution)/shard_map/ppermute | solution.py:361
  53.1 1.0 %collective-permute-done.8 = bf16[40,8,256]{2,1,0:T(8,128)(2,1)S(1)} collective-permute-done((bf16[40,8,256]{2,1,0:T(8,128)(2,1)S(1)}, bf16[40,8,256]{2,1,0:T(8,128)(2,1)S(1)}, u32[]{:S(2)}, u32[]{:S(2)}) %collective-permute-start.8) | collective-permute-done | bytes 163872 | tf_op jit(solution)/shard_map/ppermute | solution.py:361
  54.2 2.8 %collective-permute-start.9 = (bf16[20,8,256]{2,1,0:T(8,128)(2,1)S(1)}, bf16[20,8,256]{2,1,0:T(8,128)(2,1)S(1)}, u32[]{:S(2)}, u32[]{:S(2)}) collective-permute-start(bf16[20,8,256]{2,1,0:T(8,128)(2,1)S(1)} %add_convert_fusion.6), channel_id=1, source_target_pairs={{0,16},{2,18},{4,20},{6,22},{8,24},{10,26},{12,28},{14,30},{16,0},... | collective-permute-start | bytes 245768 | tf_op jit(solution)/shard_map/ppermute | solution.py:361
  57.0 1.6 %collective-permute-start.12 = (bf16[42,8,128]{2,1,0:T(8,128)(2,1)S(1)}, bf16[42,8,128]{2,1,0:T(8,128)(2,1)S(1)}, u32[]{:S(2)}, u32[]{:S(2)}) collective-permute-start(bf16[42,8,128]{2,1,0:T(8,128)(2,1)S(1)} %add_convert_fusion.5), channel_id=1, source_target_pairs={{0,8},{2,10},{4,12},{6,14},{8,0},{10,2},{12,4},{14,6},{16,24},{18,... | collective-permute-start | bytes 258056 | tf_op jit(solution)/shard_map/ppermute | solution.py:361
  58.7 2.9 %collective-permute-done.12 = bf16[42,8,128]{2,1,0:T(8,128)(2,1)S(1)} collective-permute-done((bf16[42,8,128]{2,1,0:T(8,128)(2,1)S(1)}, bf16[42,8,128]{2,1,0:T(8,128)(2,1)S(1)}, u32[]{:S(2)}, u32[]{:S(2)}) %collective-permute-start.12) | collective-permute-done | bytes 86048 | tf_op jit(solution)/shard_map/ppermute | solution.py:361
  61.6 2.0 %collective-permute-start.13 = (bf16[21,8,128]{2,1,0:T(8,128)(2,1)S(1)}, bf16[21,8,128]{2,1,0:T(8,128)(2,1)S(1)}, u32[]{:S(2)}, u32[]{:S(2)}) collective-permute-start(bf16[21,8,128]{2,1,0:T(8,128)(2,1)S(1)} %add_convert_fusion.8), channel_id=1, source_target_pairs={{0,16},{2,18},{4,20},{6,22},{8,24},{10,26},{12,28},{14,30},{16,0},... | collective-permute-start | bytes 129032 | tf_op jit(solution)/shard_map/ppermute | solution.py:361
  63.9 2.7 %collective-permute-done.13 = bf16[21,8,128]{2,1,0:T(8,128)(2,1)S(1)} collective-permute-done((bf16[21,8,128]{2,1,0:T(8,128)(2,1)S(1)}, bf16[21,8,128]{2,1,0:T(8,128)(2,1)S(1)}, u32[]{:S(2)}, u32[]{:S(2)}) %collective-permute-start.13) | collective-permute-done | bytes 43040 | tf_op jit(solution)/shard_map/ppermute | solution.py:361
  66.8 0.4 fusion.14
  67.2 1.3 %collective-permute-start.14 = (f32[20,2,641]{2,1,0:T(2,128)S(1)}, f32[20,2,641]{2,1,0:T(2,128)S(1)}, u32[]{:S(2)}, u32[]{:S(2)}) collective-permute-start(f32[20,2,641]{2,1,0:T(2,128)S(1)} %get-tuple-element.40), channel_id=1, source_target_pairs={{1,0},{3,2},{5,4},{7,6},{9,8},{11,10},{13,12},{15,14},{17,16},{19,... | collective-permute-start | bytes 307688 | tf_op jit(solution)/shard_map/ppermute | solution.py:399
  68.8 5.1 %collective-permute-done.14 = f32[20,2,641]{2,1,0:T(2,128)S(1)} collective-permute-done((f32[20,2,641]{2,1,0:T(2,128)S(1)}, f32[20,2,641]{2,1,0:T(2,128)S(1)}, u32[]{:S(2)}, u32[]{:S(2)}) %collective-permute-start.14) | collective-permute-done | bytes 102592 | tf_op jit(solution)/shard_map/ppermute | solution.py:399
  74.4 1.4 %maximum_bitcast_fusion = f32[4,2,2,20,641]{4,2,3,1,0:T(2,128)} fusion(f32[20,4,1,2,641]{4,3,0,2,1:T(2,128)S(1)} %maximum_bitcast_fusion.1, f32[20,4,1,2,1]{4,3,0,2,1:T(2,128)S(1)} %copy.28, f32[20,4,1,2,256]{4,3,1,0,2:T(2,128)S(1)} %concatenate.23, f32[20,4,1,2,256]{4,3,1,0,2:T(2,128)S(1)} %concatenate.24, f32[20,4,1,2,128]{4,3,1,0,2:T(2,128)S(1)} %bitcast.59), kind=kLoop, calls=%fused_computation | loop fusion | flops 820480 | bytes 1640960 | tf_op jit(solution)/shard_map/transpose | solution.py:409
  (46 shorter events, 2.7 us)
Async XLA Ops:
  0.6 1.6 %copy-start.1 = (bf16[4,2,32,4096]{3,2,1,0:T(8,128)(2,1)S(1)}, bf16[4,2,32,4096]{3,2,1,0:T(8,128)(2,1)}, u32[]{:S(2)}) copy-start(bf16[4,2,32,4096]{3,2,1,0:T(8,128)(2,1)} %air_ref.1) | copy-start | bytes 6291460
  2.2 5.4 %copy-start.3 = (f32[4,4,160,128]{3,2,1,0:T(8,128)S(1)}, f32[4,4,160,128]{3,2,1,0:T(8,128)}, u32[]{:S(2)}) copy-start(f32[4,4,160,128]{3,2,1,0:T(8,128)} %constant.57.clone.table_ref) | copy-start | bytes 3932164
  2.2 9.6 %copy-start.2 = (bf16[4,2,32,4096]{3,2,1,0:T(8,128)(2,1)S(1)}, bf16[4,2,32,4096]{3,2,1,0:T(8,128)(2,1)}, u32[]{:S(2)}) copy-start(bf16[4,2,32,4096]{3,2,1,0:T(8,128)(2,1)} %air_ref.1) | copy-start | bytes 6291460
  3.3 8.5 %collective-permute-start = (bf16[4,2,4096]{2,1,0:T(2,128)(2,1)}, bf16[4,2,4096]{2,1,0:T(2,128)(2,1)S(1)}, u32[]{:S(2)}, u32[]{:S(2)}) collective-permute-start(bf16[4,2,4096]{2,1,0:T(2,128)(2,1)} %get-tuple-element.18), channel_id=1, source_target_pairs={{0,2},{2,4},{4,6},{6,8},{8,10},{10,12},{12,14},{14,16},{16,18},{18... | collective-permute-start | bytes 196616 | tf_op jit(solution)/shard_map/ppermute | solution.py:319
  5.7 6.1 %collective-permute-start.1 = (bf16[4,2,4096]{2,1,0:T(2,128)(2,1)}, bf16[4,2,4096]{2,1,0:T(2,128)(2,1)S(1)}, u32[]{:S(2)}, u32[]{:S(2)}) collective-permute-start(bf16[4,2,4096]{2,1,0:T(2,128)(2,1)} %get-tuple-element.19), channel_id=1, source_target_pairs={{2,0},{4,2},{6,4},{8,6},{10,8},{12,10},{14,12},{16,14},{18,16},{20... | collective-permute-start | bytes 196616 | tf_op jit(solution)/shard_map/ppermute | solution.py:318
  7.7 15.3 %copy-start = (bf16[32,320,641]{2,1,0:T(8,128)(2,1)S(1)}, bf16[32,320,641]{2,1,0:T(8,128)(2,1)}, u32[]{:S(2)}) copy-start(bf16[32,320,641]{2,1,0:T(8,128)(2,1)} %table_ref.6) | copy-start | bytes 39383044
  11.8 1.4 %copy-start.4 = (bf16[2,32,4096]{2,1,0:T(8,128)(2,1)S(1)}, bf16[2,32,4096]{2,1,0:T(8,128)(2,1)}, u32[]{:S(2)}) copy-start(bf16[2,32,4096]{2,1,0:T(8,128)(2,1)} %kappa_ref.1) | copy-start | bytes 1572868
  26.6 6.9 %collective-permute-start.2 = (bf16[160,8,256]{2,1,0:T(8,128)(2,1)S(1)}, bf16[160,8,256]{2,1,0:T(8,128)(2,1)S(1)}, u32[]{:S(2)}, u32[]{:S(2)}) collective-permute-start(bf16[160,8,256]{2,1,0:T(8,128)(2,1)S(1)} %get-tuple-element.23), channel_id=1, source_target_pairs={{0,2},{2,0},{4,6},{6,4},{8,10},{10,8},{12,14},{14,12},{16,18},{18,... | collective-permute-start | bytes 1966088 | tf_op jit(solution)/shard_map/ppermute | solution.py:361
  33.4 2.4 %collective-permute-start.6 = (bf16[160,8,256]{2,1,0:T(8,128)(2,1)S(1)}, bf16[160,8,256]{2,1,0:T(8,128)(2,1)S(1)}, u32[]{:S(2)}, u32[]{:S(2)}) collective-permute-start(bf16[160,8,256]{2,1,0:T(8,128)(2,1)S(1)} %get-tuple-element.28), channel_id=1, source_target_pairs={{0,2},{2,0},{4,6},{6,4},{8,10},{10,8},{12,14},{14,12},{16,18},{18,... | collective-permute-start | bytes 1966088 | tf_op jit(solution)/shard_map/ppermute | solution.py:361
  33.6 10.2 %collective-permute-start.3 = (bf16[80,8,256]{2,1,0:T(8,128)(2,1)S(1)}, bf16[80,8,256]{2,1,0:T(8,128)(2,1)S(1)}, u32[]{:S(2)}, u32[]{:S(2)}) collective-permute-start(bf16[80,8,256]{2,1,0:T(8,128)(2,1)S(1)} %add_convert_fusion.1), channel_id=1, source_target_pairs={{0,4},{2,6},{4,0},{6,2},{8,12},{10,14},{12,8},{14,10},{16,20},{18,... | collective-permute-start | bytes 983048 | tf_op jit(solution)/shard_map/ppermute | solution.py:361
  35.9 11.0 %collective-permute-start.7 = (bf16[80,8,256]{2,1,0:T(8,128)(2,1)S(1)}, bf16[80,8,256]{2,1,0:T(8,128)(2,1)S(1)}, u32[]{:S(2)}, u32[]{:S(2)}) collective-permute-start(bf16[80,8,256]{2,1,0:T(8,128)(2,1)S(1)} %add_convert_fusion), channel_id=1, source_target_pairs={{0,8},{2,10},{4,12},{6,14},{8,0},{10,2},{12,4},{14,6},{16,24},{18,... | collective-permute-start | bytes 983048 | tf_op jit(solution)/shard_map/ppermute | solution.py:361
  42.3 5.5 %collective-permute-start.10 = (bf16[168,8,128]{2,1,0:T(8,128)(2,1)S(1)}, bf16[168,8,128]{2,1,0:T(8,128)(2,1)S(1)}, u32[]{:S(2)}, u32[]{:S(2)}) collective-permute-start(bf16[168,8,128]{2,1,0:T(8,128)(2,1)S(1)} %get-tuple-element.33), channel_id=1, source_target_pairs={{0,2},{2,0},{4,6},{6,4},{8,10},{10,8},{12,14},{14,12},{16,18},{18,... | collective-permute-start | bytes 1032200 | tf_op jit(solution)/shard_map/ppermute | solution.py:361
  43.8 6.4 %collective-permute-start.4 = (bf16[40,8,256]{2,1,0:T(8,128)(2,1)S(1)}, bf16[40,8,256]{2,1,0:T(8,128)(2,1)S(1)}, u32[]{:S(2)}, u32[]{:S(2)}) collective-permute-start(bf16[40,8,256]{2,1,0:T(8,128)(2,1)S(1)} %add_convert_fusion.4), channel_id=1, source_target_pairs={{0,8},{2,10},{4,12},{6,14},{8,0},{10,2},{12,4},{14,6},{16,24},{18,... | collective-permute-start | bytes 491528 | tf_op jit(solution)/shard_map/ppermute | solution.py:361
  47.0 7.1 %collective-permute-start.8 = (bf16[40,8,256]{2,1,0:T(8,128)(2,1)S(1)}, bf16[40,8,256]{2,1,0:T(8,128)(2,1)S(1)}, u32[]{:S(2)}, u32[]{:S(2)}) collective-permute-start(bf16[40,8,256]{2,1,0:T(8,128)(2,1)S(1)} %add_convert_fusion.3), channel_id=1, source_target_pairs={{0,4},{2,6},{4,0},{6,2},{8,12},{10,14},{12,8},{14,10},{16,20},{18,... | collective-permute-start | bytes 491528 | tf_op jit(solution)/shard_map/ppermute | solution.py:361
  47.8 19.0 %copy-start.5 = (f32[4]{0:T(128)S(1)}, f32[4]{0:T(128)}, u32[]{:S(2)}) copy-start(f32[4]{0:T(128)} %param.8) | copy-start | bytes 52
  47.8 9.1 %collective-permute-start.11 = (bf16[84,8,128]{2,1,0:T(8,128)(2,1)S(1)}, bf16[84,8,128]{2,1,0:T(8,128)(2,1)S(1)}, u32[]{:S(2)}, u32[]{:S(2)}) collective-permute-start(bf16[84,8,128]{2,1,0:T(8,128)(2,1)S(1)} %add_convert_fusion.2), channel_id=1, source_target_pairs={{0,4},{2,6},{4,0},{6,2},{8,12},{10,14},{12,8},{14,10},{16,20},{18,... | collective-permute-start | bytes 516104 | tf_op jit(solution)/shard_map/ppermute | solution.py:361
  50.3 8.4 %collective-permute-start.5 = (bf16[20,8,256]{2,1,0:T(8,128)(2,1)S(1)}, bf16[20,8,256]{2,1,0:T(8,128)(2,1)S(1)}, u32[]{:S(2)}, u32[]{:S(2)}) collective-permute-start(bf16[20,8,256]{2,1,0:T(8,128)(2,1)S(1)} %add_convert_fusion.7), channel_id=1, source_target_pairs={{0,16},{2,18},{4,20},{6,22},{8,24},{10,26},{12,28},{14,30},{16,0},... | collective-permute-start | bytes 245768 | tf_op jit(solution)/shard_map/ppermute | solution.py:361
  54.2 9.5 %collective-permute-start.9 = (bf16[20,8,256]{2,1,0:T(8,128)(2,1)S(1)}, bf16[20,8,256]{2,1,0:T(8,128)(2,1)S(1)}, u32[]{:S(2)}, u32[]{:S(2)}) collective-permute-start(bf16[20,8,256]{2,1,0:T(8,128)(2,1)S(1)} %add_convert_fusion.6), channel_id=1, source_target_pairs={{0,16},{2,18},{4,20},{6,22},{8,24},{10,26},{12,28},{14,30},{16,0},... | collective-permute-start | bytes 245768 | tf_op jit(solution)/shard_map/ppermute | solution.py:361
  57.0 4.6 %collective-permute-start.12 = (bf16[42,8,128]{2,1,0:T(8,128)(2,1)S(1)}, bf16[42,8,128]{2,1,0:T(8,128)(2,1)S(1)}, u32[]{:S(2)}, u32[]{:S(2)}) collective-permute-start(bf16[42,8,128]{2,1,0:T(8,128)(2,1)S(1)} %add_convert_fusion.5), channel_id=1, source_target_pairs={{0,8},{2,10},{4,12},{6,14},{8,0},{10,2},{12,4},{14,6},{16,24},{18,... | collective-permute-start | bytes 258056 | tf_op jit(solution)/shard_map/ppermute | solution.py:361
  61.6 5.0 %collective-permute-start.13 = (bf16[21,8,128]{2,1,0:T(8,128)(2,1)S(1)}, bf16[21,8,128]{2,1,0:T(8,128)(2,1)S(1)}, u32[]{:S(2)}, u32[]{:S(2)}) collective-permute-start(bf16[21,8,128]{2,1,0:T(8,128)(2,1)S(1)} %add_convert_fusion.8), channel_id=1, source_target_pairs={{0,16},{2,18},{4,20},{6,22},{8,24},{10,26},{12,28},{14,30},{16,0},... | collective-permute-start | bytes 129032 | tf_op jit(solution)/shard_map/ppermute | solution.py:361
  67.2 6.8 %collective-permute-start.14 = (f32[20,2,641]{2,1,0:T(2,128)S(1)}, f32[20,2,641]{2,1,0:T(2,128)S(1)}, u32[]{:S(2)}, u32[]{:S(2)}) collective-permute-start(f32[20,2,641]{2,1,0:T(2,128)S(1)} %get-tuple-element.40), channel_id=1, source_target_pairs={{1,0},{3,2},{5,4},{7,6},{9,8},{11,10},{13,12},{15,14},{17,16},{19,... | collective-permute-start | bytes 307688 | tf_op jit(solution)/shard_map/ppermute | solution.py:399
